TPU v7x, 128 devices: a whole 4x4x4 slice. The times are simulated.
128 devices in a mesh: angle: 8 (over y, core), tile: 16 (over z, x).
Axes of the slice: x: 4, y: 4, z: 4, core: 2. Of those that a mesh axis runs over, the one named last changes fastest.
Arguments:
- psi: float32 [2, 8, 160, 2048], P(None, 'angle', None, 'tile'), may hold values from -6 to 6
- target: float32 [2, 8, 160, 2048], P(None, 'angle', None, 'tile'), may hold values from -6 to 6
- probe: float32 [2, 128, 128], replicated, may hold values from -4.2 to 4.2
- data: float32 [8, 16, 16, 128, 128], P('angle', 'tile'), may hold values from 0.1 to 10
- pos_z: int32 [8, 16, 16], P('angle', 'tile'), may hold values from 0 to 32
- pos_x: int32 [8, 16, 16], P('angle', 'tile'), may hold values from 0 to 127
- counts: int32 [8, 16], P('angle', 'tile'), may hold values from 1 to 16, as said below
- shears: float32 [8], P('angle'), may hold values from -1 to 1
Outputs:
- psi_new: float32 [2, 8, 160, 2048], P(None, 'angle', None, 'tile')
- probe_new: float32 [2, 128, 128], replicated
- tomo_grad: bfloat16 [2, 160, 256, 2048], P(None, 'tile', 'angle')
Inputs may be any that keep to these rules, and one draw needn't show every extreme that they name: counts[a, t] positions of angle a lie in tile t, in slots 0 to counts[a, t] - 1; later slots are unused. Some tile of some angle has exactly 16 in every draw.
All inputs are finite; a program needn't handle non-finite values.
Results may differ from a plain program's by a relative error of at most 0.001.
Values sent between devices are 32-bit elements; how exact they have to be, the bound alone decides.
A program may use at most 192 MiB of HBM per device.

v0:
```python
import math

import jax
import jax.numpy as jnp
from jax import lax
from jax.sharding import PartitionSpec as P

YB = 32
ITERS = 2


ALPHA = 0.004
RHO = 5.0
PROBE_STEP = 0.02
HIGHEST = lax.Precision.HIGHEST


def extended_2(block, sides, width):
    for axis, dim in sides:
        count = lax.axis_size(axis)
        forward = [(i, i + 1) for i in range(count - 1)]
        backward = [(target, source) for source, target in forward]
        low = lax.ppermute(
            lax.slice_in_dim(block, block.shape[dim] - width, None, axis=dim), axis, forward
        )
        high = lax.ppermute(lax.slice_in_dim(block, 0, width, axis=dim), axis, backward)
        block = jnp.concatenate([low, block, high], axis=dim)
    return block


def twin_einsum(pattern, left_real, left_imag, right_real, right_imag):
    real_part = jnp.einsum(pattern, left_real, right_real, precision=HIGHEST) - jnp.einsum(
        pattern, left_imag, right_imag, precision=HIGHEST
    )
    imag_part = jnp.einsum(pattern, left_real, right_imag, precision=HIGHEST) + jnp.einsum(
        pattern, left_imag, right_real, precision=HIGHEST
    )
    return (real_part, imag_part)


def phase_table(integers, modulus, orient):
    radians = 2.0 * math.pi / modulus * (integers % modulus).astype(jnp.float32)
    return (jnp.cos(radians), orient * jnp.sin(radians))


def square_table(length, orient):
    counter = lax.iota(jnp.int32, length)
    return phase_table(counter[:, None] * counter[None, :], length, orient)


def twiddle_table(inner, outer, orient):
    coarse = lax.iota(jnp.int32, outer)
    fine = lax.iota(jnp.int32, inner)
    return phase_table(coarse[:, None] * fine[None, :], inner * outer, orient)


def forward_rows(values_real, values_imag, inner, outer):
    leading = values_real.shape[:-1]
    shaped_real = values_real.reshape(leading + (outer, inner))
    shaped_imag = values_imag.reshape(leading + (outer, inner))
    outer_real, outer_imag = square_table(outer, -1.0)
    inner_real, inner_imag = square_table(inner, -1.0)
    twist_real, twist_imag = twiddle_table(inner, outer, -1.0)
    first_real, first_imag = twin_einsum(
        "...ab,ac->...cb", shaped_real, shaped_imag, outer_real, outer_imag
    )
    turned_real = first_real * twist_real - first_imag * twist_imag
    turned_imag = first_real * twist_imag + first_imag * twist_real
    final_real, final_imag = twin_einsum(
        "...cb,bd->...cd", turned_real, turned_imag, inner_real, inner_imag
    )
    return (
        final_real.reshape(leading + (inner * outer,)),
        final_imag.reshape(leading + (inner * outer,)),
    )


def inverse_rows(values_real, values_imag, inner, outer):
    leading = values_real.shape[:-1]
    shaped_real = values_real.reshape(leading + (outer, inner))
    shaped_imag = values_imag.reshape(leading + (outer, inner))
    outer_real, outer_imag = square_table(outer, 1.0)
    inner_real, inner_imag = square_table(inner, 1.0)
    twist_real, twist_imag = twiddle_table(inner, outer, 1.0)
    first_real, first_imag = twin_einsum(
        "...ab,bc->...ac", shaped_real, shaped_imag, inner_real, inner_imag
    )
    turned_real = first_real * twist_real - first_imag * twist_imag
    turned_imag = first_real * twist_imag + first_imag * twist_real
    final_real, final_imag = twin_einsum(
        "...ac,ad->...dc", turned_real, turned_imag, outer_real, outer_imag
    )
    scale = 1.0 / (inner * outer)
    return (
        final_real.reshape(leading + (inner * outer,)) * scale,
        final_imag.reshape(leading + (inner * outer,)) * scale,
    )


def pattern_transform(field_real, field_imag, table_real, table_imag):
    middle_real, middle_imag = twin_einsum(
        "mn,pnq->pmq", table_real, table_imag, field_real, field_imag
    )
    return twin_einsum("pmq,qr->pmr", middle_real, middle_imag, table_real, table_imag)


def shards(psi, target, probe, data, pos_z, pos_x, counts, shears):
    angle_count = psi.shape[1]
    rows_total = psi.shape[2]
    tile_width = psi.shape[3]
    patch_side = probe.shape[1]
    half = patch_side // 2
    slot_count = data.shape[2]
    tiles = lax.axis_size("tile")
    wide_cols = tile_width + patch_side
    norm_factor = 1.0 / math.sqrt(patch_side)
    fwd_real, fwd_imag = square_table(patch_side, -1.0)
    inv_real, inv_imag = square_table(patch_side, 1.0)
    fwd_real, fwd_imag = (fwd_real * norm_factor, fwd_imag * norm_factor)
    inv_real, inv_imag = (inv_real * norm_factor, inv_imag * norm_factor)
    slot_mask = (
        (lax.iota(jnp.int32, slot_count)[None, :] < counts[:, 0][:, None])
        .astype(jnp.float32)
        .reshape(-1)
    )
    angle_ids = jnp.repeat(jnp.arange(angle_count, dtype=jnp.int32), slot_count)
    starts_z = pos_z.reshape(-1)
    starts_x = pos_x.reshape(-1)
    data_flat = data.reshape(-1, patch_side, patch_side)
    local_count = jnp.sum(counts).astype(jnp.float32)
    zero_index = jnp.zeros((), jnp.int32)
    window_index = lax.iota(jnp.int32, patch_side)
    place_cols = (
        lax.iota(jnp.int32, wide_cols)[None, None, :]
        == (starts_x[:, None] + window_index[None, :])[:, :, None]
    ).astype(jnp.float32)
    place_rows = (
        lax.iota(jnp.int32, rows_total)[None, None, :]
        == (starts_z[:, None] + window_index[None, :])[:, :, None]
    ).astype(jnp.float32)
    place_rows = place_rows.reshape(angle_count, slot_count, patch_side, rows_total)
    field = psi
    probe_now = probe
    for step in range(ITERS):
        extended = extended_2(field, (("tile", 3),), half)

        def cut_patch(angle_id, start_z, start_x):
            return lax.dynamic_slice(
                extended, (zero_index, angle_id, start_z, start_x), (2, 1, patch_side, patch_side)
            )[:, 0]

        patches = jax.vmap(cut_patch)(angle_ids, starts_z, starts_x)
        patch_real = patches[:, 0]
        patch_imag = patches[:, 1]
        exit_real = probe_now[0] * patch_real - probe_now[1] * patch_imag
        exit_imag = probe_now[0] * patch_imag + probe_now[1] * patch_real
        far_real, far_imag = pattern_transform(exit_real, exit_imag, fwd_real, fwd_imag)
        misfit = (far_real * far_real + far_imag * far_imag - data_flat) * slot_mask[:, None, None]
        back_real, back_imag = pattern_transform(
            misfit * far_real, misfit * far_imag, inv_real, inv_imag
        )
        grad_real = probe_now[0] * back_real + probe_now[1] * back_imag
        grad_imag = probe_now[0] * back_imag - probe_now[1] * back_real
        probe_part = jnp.stack(
            [
                jnp.sum(patch_real * back_real + patch_imag * back_imag, 0),
                jnp.sum(patch_real * back_imag - patch_imag * back_real, 0),
            ]
        )
        stacked_grad = jnp.stack([grad_real, grad_imag], 1)
        widened = jnp.einsum("spre,sew->psrw", stacked_grad, place_cols, precision=HIGHEST)
        widened = widened.reshape(2, angle_count, slot_count, patch_side, wide_cols)
        total = jnp.einsum("pasrw,asrz->pazw", widened, place_rows, precision=HIGHEST)
        own = total[:, :, :, half : half + tile_width]
        rims = jnp.concatenate([total[:, :, :, :half], total[:, :, :, half + tile_width :]], 3)
        returned = extended_2(rims, (("tile", 3),), half)
        own = own.at[:, :, :, :half].add(returned[:, :, :, :half])
        own = own.at[:, :, :, tile_width - half :].add(returned[:, :, :, half + patch_side :])
        probe_grad, count_total = lax.psum((probe_part, local_count), ("angle", "tile"))
        new_field = field - ALPHA * (own + RHO * (field - target))
        probe_now = probe_now - PROBE_STEP * probe_grad / count_total
        field = new_field
    misfit_rows = target - field
    every_angle, all_shears = (
        lax.all_gather(misfit_rows, "angle", axis=1, tiled=True),
        lax.all_gather(shears, "angle", axis=0, tiled=True),
    )
    slab = lax.all_to_all(every_angle, "tile", split_axis=2, concat_axis=3, tiled=True)
    spec_real, spec_imag = forward_rows(slab[0], slab[1], tile_width, tiles)
    spectra = jnp.stack([spec_real, spec_imag])
    width = spectra.shape[-1]
    total_angles = all_shears.shape[0]
    band_rows = YB
    beam_rows = band_rows * lax.axis_size("angle")
    first_row = lax.axis_index("angle") * band_rows - beam_rows // 2
    offsets = first_row + lax.iota(jnp.int32, band_rows)
    position = lax.iota(jnp.int32, width)
    frequency = position // tile_width + tiles * (position % tile_width)
    signed = jnp.where(frequency < width // 2, frequency, frequency - width)
    product = (offsets[:, None] * signed[None, :]).astype(jnp.float32)
    theta = product[:, None, :] * all_shears[None, :, None] * (2.0 * math.pi / width)
    shift_real = jnp.cos(theta)
    shift_imag = jnp.sin(theta)
    summed_real, summed_imag = twin_einsum(
        "yak,azk->zyk", shift_real, shift_imag, spectra[0], spectra[1]
    )
    image_real, image_imag = inverse_rows(summed_real, summed_imag, tile_width, tiles)
    tomo = jnp.stack([image_real, image_imag]) / total_angles
    return (field, probe_now, tomo.astype(jnp.bfloat16))


def solution(mesh):
    in_specs = (
        P(None, "angle", None, "tile"),
        P(None, "angle", None, "tile"),
        P(),
        P("angle", "tile", None, None, None),
        P("angle", "tile", None),
        P("angle", "tile", None),
        P("angle", "tile"),
        P("angle"),
    )
    out_specs = (P(None, "angle", None, "tile"), P(), P(None, "tile", "angle", None))
    return jax.shard_map(shards, mesh=mesh, in_specs=in_specs, out_specs=out_specs, check_vma=False)
```

profile of v0, /device:TPU:1, one launch (start us, length us, event | category | flops | bytes accessed | tf_op | source)
XLA Modules:
  0.0 910.7 jit_solution(7082404497665718578)
XLA Ops:
  8.3 3.9 collective-permute-start
  14.2 69.6 %psum.25 = f32[]{:T(128)} all-reduce(f32[]{:T(128)S(6)} %convert_element_type.156), channel_id=1, replica_groups=mesh['angle'=8,'tile'=16] {'angle','tile'}, use_global_device_ids=true, to_apply=%region_3.4 | all-reduce | flops 1 | bytes 8 | tf_op jit(solution)/shard_map/psum | solution.py:179
  88.2 32.2 %while.6 = (s32[]{:T(128)}, f32[2,1,160,256]{3,2,1,0:T(8,128)S(1)}, s32[16,4]{0,1:T(4,128)S(1)}, f32[16,2,1,128,128]{4,3,0,1,2:T(8,128)S(1)}, s32[]{:T(128)}) while((s32[]{:T(128)}, f32[2,1,160,256]{3,2,1,0:T(8,128)S(1)}, s32[16,4]{0,1:T(4,128)S(1)}, f32[16,2,1,128,128]{4,3,0,1,2:T(8,128)S(1)}, s32[]{:T(128)}) %tuple.80), condition=%wide.while_cond.4, body=%wide.while_body.4.sunk | while | flops 2 | bytes 262277 | solution.py:148
  130.4 2.0 fusion.42
  132.5 2.4 convolution_subtract_fusion.8
  134.9 2.3 fusion.61
  145.0 2.1 fusion.137
  151.0 3.7 add_reduce_fusion.1
  155.5 3.7 fusion.25
  159.2 2.6 fusion.47
  163.3 4.0 collective-permute-start.2
  167.3 127.2 %all-reduce.4.cloned.1.call-done = f32[2,128,128]{2,1,0:T(8,128)} async-done(((f32[2,128,128]{2,1,0:T(8,128)}), f32[2,128,128]{2,1,0:T(8,128)}) %all-reduce.4.cloned.1.call-update) | async-done | bytes 131088 | tf_op jit(solution)/shard_map/psum | solution.py:179
  298.0 2.4 collective-permute-start.4
  302.6 3.8 collective-permute-done.5
  307.5 48.2 %while.7 = (s32[]{:T(128)}, f32[2,1,160,256]{3,2,1,0:T(8,128)}, s32[16,4]{0,1:T(4,128)S(1)}, f32[16,2,1,128,128]{4,3,0,1,2:T(8,128)S(1)}, s32[]{:T(128)}) while((s32[]{:T(128)}, f32[2,1,160,256]{3,2,1,0:T(8,128)}, s32[16,4]{0,1:T(4,128)S(1)}, f32[16,2,1,128,128]{4,3,0,1,2:T(8,128)S(1)}, s32[]{:T(128)}) %tuple.92), condition=%wide.while_cond.5, body=%wide.while_body.5.sunk | while | flops 2 | bytes 262277 | solution.py:148
  308.2 2.3 bitcast_dynamic-update-slice_fusion.5
  311.2 2.3 bitcast_dynamic-update-slice_fusion.5
  314.1 2.3 bitcast_dynamic-update-slice_fusion.5
  317.1 2.3 bitcast_dynamic-update-slice_fusion.5
  320.1 2.3 bitcast_dynamic-update-slice_fusion.5
  323.1 2.3 bitcast_dynamic-update-slice_fusion.5
  326.1 2.3 bitcast_dynamic-update-slice_fusion.5
  329.1 2.3 bitcast_dynamic-update-slice_fusion.5
  332.1 2.3 bitcast_dynamic-update-slice_fusion.5
  335.1 2.3 bitcast_dynamic-update-slice_fusion.5
  338.0 2.3 bitcast_dynamic-update-slice_fusion.5
  341.0 2.3 bitcast_dynamic-update-slice_fusion.5
  344.0 2.3 bitcast_dynamic-update-slice_fusion.5
  347.0 2.3 bitcast_dynamic-update-slice_fusion.5
  350.0 2.3 bitcast_dynamic-update-slice_fusion.5
  353.0 2.3 bitcast_dynamic-update-slice_fusion.5
  367.7 2.1 convolution_subtract_fusion.4
  369.9 2.3 fusion.59
  379.9 2.3 fusion.125
  386.2 2.4 add_reduce_fusion
  388.6 2.2 fusion.29
  390.8 2.7 fusion.52
  393.7 4.2 collective-permute-start.6
  400.8 3.3 collective-permute-done.7
  407.9 14.7 %all-reduce = f32[8]{0:T(128)S(1)} all-reduce(f32[8]{0:T(128)S(1)} %dynamic-update-slice.16), channel_id=1, replica_groups=mesh['angle'=8,'tile'=16] {'angle'}, use_global_device_ids=true, to_apply=%add | all-reduce | flops 8 | bytes 64
  422.6 12.2 %all-gather.2.cloned.1.call-done = f32[2,8,160,128]{3,2,0,1:T(8,128)} async-done(((f32[2,1,160,128]{3,2,0,1:T(8,128)}), f32[2,8,160,128]{3,2,0,1:T(8,128)}) %all-gather.2.cloned.1.call-update) | async-done | bytes 1310736 | tf_op jit(solution)/shard_map/all_gather | solution.py:185
  434.7 3.4 copy.212
  438.1 6.8 all-to-all-start
  446.2 146.8 %all-reduce.6.cloned.1.call-done = f32[2,128,128]{2,1,0:T(8,128)} async-done(((f32[2,128,128]{2,1,0:T(8,128)}), f32[2,128,128]{2,1,0:T(8,128)}) %all-reduce.6.cloned.1.call-update) | async-done | bytes 131088 | tf_op jit(solution)/shard_map/psum | solution.py:179
  593.1 2.1 divide_subtract_fusion
  602.6 4.5 copy.276
  607.2 4.5 copy.275
  611.7 57.4 %fusion.2 = f32[2048,10,32]{2,1,0:T(8,128)} fusion(f32[8,10,2048]{1,0,2:T(8,128)} %bitcast.410, f32[8]{0:T(128)S(1)} %all-reduce, f32[32,2048]{0,1:T(8,128)S(1)} %copy.216), kind=kOutput, calls=%fused_computation.9 | convolution fusion | flops 63963136 | bytes 3538976 | tf_op jit(solution)/shard_map/yak,azk->zyk/dot_general | solution.py:35
  669.1 54.3 %fusion.4 = f32[2048,10,32]{2,1,0:T(8,128)S(1)} fusion(f32[8,10,2048]{1,0,2:T(8,128)S(1)} %bitcast.409, f32[8]{0:T(128)S(1)} %all-reduce, f32[32,2048]{0,1:T(8,128)S(1)} %copy.216), kind=kOutput, calls=%fused_computation.10 | convolution fusion | flops 63963136 | bytes 3538976 | tf_op jit(solution)/shard_map/yak,azk->zyk/dot_general | solution.py:32
  723.5 56.6 %convolution_subtract_fusion = f32[2048,10,32]{2,1,0:T(8,128)} fusion(f32[2048,10,32]{2,1,0:T(8,128)S(1)} %fusion.4, f32[8,10,2048]{1,0,2:T(8,128)S(1)} %bitcast.413, f32[8]{0:T(128)S(1)} %all-reduce, f32[32,2048]{0,1:T(8,128)S(1)} %copy.216), kind=kOutput, calls=%fused_computation.5 | convolution fusion | flops 64618496 | bytes 6160416 | tf_op jit(solution)/shard_map/yak,azk->zyk/dot_general | solution.py:32
  780.1 9.4 %copy.220 = f32[10,32,16,128]{3,2,1,0:T(8,128)} copy(f32[10,32,16,128]{1,0,3,2:T(8,128)} %bitcast.415) | data formatting | bytes 5242880 | tf_op jit(solution)/shard_map/reshape | solution.py:80
  789.5 5.8 fusion.92
  795.4 4.0 fusion.96
  799.3 58.7 %convolution_add_fusion = f32[2048,10,32]{2,1,0:T(8,128)} fusion(f32[2048,10,32]{2,1,0:T(8,128)} %fusion.2, f32[8,10,2048]{1,0,2:T(8,128)} %bitcast.408, f32[8]{0:T(128)S(1)} %all-reduce, f32[32,2048]{0,1:T(8,128)S(1)} %copy.216), kind=kOutput, calls=%fused_computation.4 | convolution fusion | flops 64618496 | bytes 6160416 | tf_op jit(solution)/shard_map/yak,azk->zyk/dot_general | solution.py:35
  858.0 9.4 %copy.223 = f32[10,32,16,128]{3,2,1,0:T(8,128)} copy(f32[10,32,16,128]{1,0,3,2:T(8,128)} %bitcast.414) | data formatting | bytes 5242880 | tf_op jit(solution)/shard_map/reshape | solution.py:81
  867.5 5.1 convolution_add_fusion.1
  872.6 2.6 convolution_subtract_fusion.1
  875.2 2.5 fusion.65
  877.7 4.0 fusion.66
  881.7 4.3 multiply_bitcast_fusion
  886.0 3.8 mul.1050
  889.7 6.5 multiply_bitcast_fusion.1
  896.2 3.9 mul.1047
  900.1 3.9 fusion.8
  (203 shorter events, 117.5 us)
Async XLA Ops:
  7.2 287.4 %all-reduce.4.cloned.1.call-start = ((), (), s32[]{:S(2)}) async-start(), calls=%async_computation.1 | async-start | bytes 262144 | tf_op jit(solution)/shard_map/psum | solution.py:179
  8.3 78.6 %collective-permute-start = (f32[2,1,160,64]{3,2,1,0:T(8,128)S(1)}, f32[2,1,160,64]{3,2,1,0:T(8,128)S(1)}, u32[]{:S(2)}, u32[]{:S(2)}) collective-permute-start(f32[2,1,160,64]{3,2,1,0:T(8,128)S(1)} %get-tuple-element.139), channel_id=1, source_target_pairs={{0,1},{1,2},{2,3},{3,4},{4,5},{5,6},{6,7},{7,8},{8,9},{9,10},{10,1... | collective-permute-start | bytes 245768 | tf_op jit(solution)/shard_map/ppermute | solution.py:23
  12.3 74.6 %collective-permute-start.1 = (f32[2,1,160,64]{3,2,1,0:T(8,128)S(1)}, f32[2,1,160,64]{3,2,1,0:T(8,128)S(1)}, u32[]{:S(2)}, u32[]{:S(2)}) collective-permute-start(f32[2,1,160,64]{3,2,1,0:T(8,128)S(1)} %get-tuple-element.140), channel_id=1, source_target_pairs={{1,0},{2,1},{3,2},{4,3},{5,4},{6,5},{7,6},{8,7},{9,8},{10,9},{11,1... | collective-permute-start | bytes 245768 | tf_op jit(solution)/shard_map/ppermute | solution.py:26
  130.4 4.5 copy-start.6
  155.4 279.3 %all-gather.2.cloned.1.call-start = ((), (), s32[]{:S(2)}) async-start(), calls=%async_computation.3 | async-start | bytes 1474560 | tf_op jit(solution)/shard_map/all_gather | solution.py:185
  159.2 135.4 %copy-start.12 = (f32[2,128,128]{2,1,0:T(8,128)S(1)}, f32[2,128,128]{2,1,0:T(8,128)}, u32[]{:S(2)}) copy-start(f32[2,128,128]{2,1,0:T(8,128)} %param.18) | copy-start | bytes 393220
  161.8 136.0 %copy-start.7 = (f32[2,1,160,128]{3,2,1,0:T(8,128)S(1)}, f32[2,1,160,128]{3,2,1,0:T(8,128)}, u32[]{:S(2)}) copy-start(f32[2,1,160,128]{3,2,1,0:T(8,128)} %param.16) | copy-start | bytes 491524
  161.8 136.0 %copy-start.10 = (f32[2,1,160,128]{3,2,1,0:T(8,128)S(1)}, f32[2,1,160,128]{3,2,1,0:T(8,128)}, u32[]{:S(2)}) copy-start(f32[2,1,160,128]{3,2,1,0:T(8,128)} %param.17) | copy-start | bytes 491524
  162.0 134.7 %collective-permute-start.3 = (f32[2,1,160,64]{3,2,0,1:T(8,128)S(1)}, f32[2,1,160,64]{3,2,0,1:T(8,128)S(1)}, u32[]{:S(2)}, u32[]{:S(2)}) collective-permute-start(f32[2,1,160,64]{3,2,0,1:T(8,128)S(1)} %get-tuple-element.135), channel_id=1, source_target_pairs={{1,0},{2,1},{3,2},{4,3},{5,4},{6,5},{7,6},{8,7},{9,8},{10,9},{11,1... | collective-permute-start | bytes 245768 | tf_op jit(solution)/shard_map/ppermute | solution.py:26
  163.3 132.8 %collective-permute-start.2 = (f32[2,1,160,64]{3,2,0,1:T(8,128)S(1)}, f32[2,1,160,64]{3,2,0,1:T(8,128)S(1)}, u32[]{:S(2)}, u32[]{:S(2)}) collective-permute-start(f32[2,1,160,64]{3,2,0,1:T(8,128)S(1)} %get-tuple-element.136), channel_id=1, source_target_pairs={{0,1},{1,2},{2,3},{3,4},{4,5},{5,6},{6,7},{7,8},{8,9},{9,10},{10,1... | collective-permute-start | bytes 245768 | tf_op jit(solution)/shard_map/ppermute | solution.py:23
  296.1 10.3 %copy-start.8 = (f32[2,128,128]{2,1,0:T(8,128)}, f32[2,128,128]{2,1,0:T(8,128)S(1)}, u32[]{:S(2)}) copy-start(f32[2,128,128]{2,1,0:T(8,128)S(1)} %divide_subtract_fusion.1) | copy-start | bytes 393220
  298.0 4.6 collective-permute-start.4
  300.3 6.1 collective-permute-start.5
  390.8 14.3 %copy-start.11 = (f32[2,1,160,128]{3,2,1,0:T(8,128)S(1)}, f32[2,1,160,128]{3,2,1,0:T(8,128)}, u32[]{:S(2)}) copy-start(f32[2,1,160,128]{3,2,1,0:T(8,128)} %param.17) | copy-start | bytes 491524
  393.6 13.0 %copy-start.13 = (u32[128]{0:T(128)S(1)}, u32[128]{0:T(128)}, u32[]{:S(2)}) copy-start(u32[128]{0:T(128)} %constant.266) | copy-start | bytes 1540
  393.7 6.5 collective-permute-start.6
  398.0 6.1 collective-permute-start.7
  438.1 154.9 %copy-start.9 = (f32[2,128,128]{2,1,0:T(8,128)S(1)}, f32[2,128,128]{2,1,0:T(8,128)}, u32[]{:S(2)}) copy-start(f32[2,128,128]{2,1,0:T(8,128)} %copy-done.8) | copy-start | bytes 393220
  438.1 157.1 %all-to-all-start = ((f32[2,8,160,128]{3,0,1,2:T(2,128)}), f32[2,8,160,128]{3,0,1,2:T(2,128)S(1)}, u32[]{:S(2)}, u32[]{:S(2)}) async-start(f32[2,8,160,128]{3,0,1,2:T(2,128)} %copy.212), calls=%async_computation | async-start | bytes 2621440 | tf_op jit(solution)/shard_map/all_to_all | solution.py:188
  444.9 148.1 %all-reduce.6.cloned.1.call-start = ((), (), s32[]{:S(2)}) async-start(), calls=%async_computation.2 | async-start | bytes 262144 | tf_op jit(solution)/shard_map/psum | solution.py:179
  611.7 57.4 %copy-start = (f32[8,10,16,128]{1,0,3,2:T(8,128)S(1)}, f32[8,10,16,128]{1,0,3,2:T(8,128)}, u32[]{:S(2)}) copy-start(f32[8,10,16,128]{1,0,3,2:T(8,128)} %copy.276) | copy-start | bytes 1966084
  611.7 111.8 %slice-start = ((s8[8388608]{0:T(1024)(128)(4,1)}), s8[4194304]{0:T(1024)(128)(4,1)S(1)}, s32[]{:S(2)}) async-start(s8[8388608]{0:T(1024)(128)(4,1)} %bitcast.411), calls=%async_computation.4 | async-start | bytes 8388608
  669.1 54.4 %slice-start.1 = ((s8[8388608]{0:T(1024)(128)(4,1)}), s8[4194304]{0:T(1024)(128)(4,1)S(1)}, s32[]{:S(2)}) async-start(s8[8388608]{0:T(1024)(128)(4,1)} %bitcast.411), calls=%async_computation.5 | async-start | bytes 8388608
  789.5 5.9 copy-start.2
  867.5 5.1 copy-start.3
  867.5 5.1 copy-start.4
  875.2 6.5 copy-start.1
  896.2 3.9 copy-start.5
Sparse Core Ops, SparseCore 0:
  155.6 138.9 all-reduce.3
  406.0 28.6 all-gather.1
  450.5 142.5 all-reduce.5
where the time goes:
time: 922 us; the launch traced here: 911 us
  matrix products  346 us (38%)
  waiting for transfers between devices  295 us (32%)
  local copies, waits for them, and re-layouts  127 us (14%)
  blocking collectives  84.3 us (9%)
  starting transfers between devices  26.6 us (3%)
  between operations  16.1 us (2%)
  other arithmetic  14.5 us (2%)
    psum x2, waiting for transfers between devices, shards(): lax.psum((probe_part, local_count), ('angle', 'tile'))  274 us
    dot_general x13, matrix products, twin_einsum(): jnp.einsum(pattern, left_imag, right_real, precision=HIGHEST)  86.1 us
    dot_general x13, matrix products, twin_einsum(): jnp.einsum(pattern, left_imag, right_imag, precision=HIGHEST)  85.9 us
    dot_general x13, matrix products, twin_einsum(): jnp.einsum(pattern, left_real, right_imag, precision=HIGHEST)  83.1 us
    dot_general x13, matrix products, twin_einsum(): jnp.einsum(pattern, left_real, right_real, precision=HIGHEST)  80.1 us
    gather x96, local copies, waits for them, and re-layouts  79.4 us
    psum x1, blocking collectives, shards(): lax.psum((probe_part, local_count), ('angle', 'tile'))  69.6 us
  transfers between devices with their start and end apart: 12, of which 7 were waited for; matrix products, arithmetic and copies ran while one was open for 2% of the time, Pallas kernels for 0%

commit v1 on v0

v1 whole, which is shorter than its diff:
```python
import functools
import math

import jax
import jax.numpy as jnp
import numpy as np
from jax import lax
from jax.experimental import pallas as pl
from jax.experimental.pallas import tpu as pltpu
from jax.sharding import PartitionSpec as P

ITERS = 2
ALPHA = 0.004
RHO = 5.0
PROBE_STEP = 0.02

ANG = 8
TILES = 16
PS = 128
TW = 128
ROWS = 160
CAP = 16
HALF = 64
WIDE = 256
ZS = ROWS // TILES
YB = 32
H = 2048
CHUNK = 2 * PS // ANG
CROWS = CHUNK + 8

F32 = jnp.float32
BF16 = jnp.bfloat16
MESH = pl.DeviceIdType.MESH
VMEM = pl.BlockSpec(memory_space=pltpu.VMEM)
SMEM = pl.BlockSpec(memory_space=pltpu.SMEM)
VLIMIT = 60 * 1024 * 1024


def dft_block(length, scale):
    index = np.arange(length)
    turns = (index[:, None] * index[None, :]) % length
    angle = -2.0 * math.pi * turns / length
    real, imag = np.cos(angle) * scale, np.sin(angle) * scale
    return np.block([[real, imag], [-imag, real]])


def split_const(matrix):
    high = matrix.astype(BF16)
    low = (matrix - high.astype(np.float64)).astype(BF16)
    return high, low


def right_table(matrix):
    high, low = split_const(matrix)
    return np.concatenate([high, high, low], axis=0)


def left_table(matrix):
    high, low = split_const(matrix)
    return np.concatenate([high, high, low], axis=1)


def turn_table(orient):
    angle = orient * 2.0 * math.pi * np.arange(TILES)[:, None] * np.arange(TW)[None, :] / H
    return np.stack([np.cos(angle), np.sin(angle)]).astype(np.float32)


def split(value):
    high = value.astype(BF16)
    low = (value - high.astype(F32)).astype(BF16)
    return high, low


def dot_right(value, table):
    high, low = split(value)
    return jnp.dot(jnp.concatenate([high, low, high], axis=1), table, preferred_element_type=F32)


def dot_left(table, value):
    high, low = split(value)
    return jnp.dot(table, jnp.concatenate([high, low, high], axis=0), preferred_element_type=F32)


def times(left, right):
    return left[0] * right[0] - left[1] * right[1], left[0] * right[1] + left[1] * right[0]


def four(items, orient):
    (ar, ai), (br, bi), (cr, ci), (dr, di) = items
    sr, si, ur, ui = ar + cr, ai + ci, ar - cr, ai - ci
    pr, pi, qr, qi = br + dr, bi + di, br - dr, bi - di
    first = (sr + pr, si + pi)
    third = (sr - pr, si - pi)
    plus = (ur - qi, ui + qr)
    minus = (ur + qi, ui - qr)
    return [first, plus, third, minus] if orient > 0 else [first, minus, third, plus]


def sixteen(items, orient):
    columns = []
    for fine in range(4):
        partial = four([items[4 * coarse + fine] for coarse in range(4)], orient)
        for order in range(1, 4):
            step = fine * order
            if step:
                angle = orient * 2.0 * math.pi * step / 16
                partial[order] = times(partial[order], (math.cos(angle), math.sin(angle)))
        columns.append(partial)
    result = [None] * 16
    for low in range(4):
        finished = four([columns[fine][low] for fine in range(4)], orient)
        for high in range(4):
            result[low + 4 * high] = finished[high]
    return result


def lanes(shape):
    return lax.broadcasted_iota(jnp.int32, shape, len(shape) - 1)


def sublanes(shape):
    return lax.broadcasted_iota(jnp.int32, shape, len(shape) - 2)


def place():
    return lax.axis_index("angle"), lax.axis_index("tile")


def meet(peers):
    barrier = pltpu.get_barrier_semaphore()
    for peer in peers:
        pl.semaphore_signal(barrier, inc=1, device_id=peer, device_id_type=MESH)
    pl.semaphore_wait(barrier, len(peers))


def send(source, target, sems, slot, peer):
    copy = pltpu.make_async_remote_copy(
        src_ref=source,
        dst_ref=target,
        send_sem=sems.at[0, slot],
        recv_sem=sems.at[1, slot],
        device_id=peer,
        device_id_type=MESH,
    )
    copy.start()
    return copy


def angle_peers(angle, tile):
    return [((angle + step) % ANG, tile) for step in range(1, ANG)]


def tile_peers(angle, tile):
    return [(angle, (tile + step) % TILES) for step in range(1, TILES)]


def neighbours(angle, tile):
    return (angle, (tile + TILES - 1) % TILES), (angle, (tile + 1) % TILES)


def halo_kernel(psi, target, from_left, from_right, pack_left, pack_right, sems):
    angle, tile = place()
    left, right = neighbours(angle, tile)
    low = lanes((ROWS, TW)) < HALF
    for index, source in enumerate((psi, target)):
        real, imag = source[0], source[1]
        pack_left[index] = jnp.where(low, real, pltpu.roll(imag, HALF, 1))
        pack_right[index] = jnp.where(low, pltpu.roll(real, HALF, 1), imag)
    meet([left, right])
    copies = []
    copies.append(send(pack_left, from_right, sems, 0, left))
    copies.append(send(pack_right, from_left, sems, 1, right))
    for copy in copies:
        copy.wait()


def start_edges(grad, from_left, from_right, sems, angle, tile):
    left, right = neighbours(angle, tile)
    return [
        send(grad.at[0], from_right, sems, 0, left),
        send(grad.at[1], from_left, sems, 1, right),
    ]


def start_first(parts, landed, sems, angle, tile):
    return [
        send(parts.at[(angle + step) % ANG], landed.at[step], sems, step, ((angle + step) % ANG, tile))
        for step in range(1, ANG)
    ]


def finish_first(copies, parts, landed, angle):
    for copy in copies:
        copy.wait()
    total = parts[angle]
    for step in range(1, ANG):
        total = total + landed[step]
    return total


def start_second(source, landed, sems, angle, tile):
    return [
        send(source, landed.at[tile], sems, step, (angle, (tile + step) % TILES))
        for step in range(1, TILES)
    ]


def finish_second(copies, source, landed, tile):
    landed[tile] = source[...]
    for copy in copies:
        copy.wait()
    total = landed[0]
    for index in range(1, TILES):
        total = total + landed[index]
    return total


def start_third(source, gathered, sems, angle, tile):
    return [
        send(source, gathered.at[angle], sems, step, ((angle + step) % ANG, tile))
        for step in range(1, ANG)
    ]


def exchange_kernel(
    grad, parts, from_left, from_right, first_out, gathered,
    landed_first, first_sum, landed_second, second_sum, edge_sems, first_sems, second_sems, third_sems,
):
    angle, tile = place()
    meet(angle_peers(angle, tile) + tile_peers(angle, tile))
    first = start_first(parts, landed_first, first_sems, angle, tile)
    edges = start_edges(grad, from_left, from_right, edge_sems, angle, tile)
    first_sum[...] = finish_first(first, parts, landed_first, angle)
    second = start_second(first_sum, landed_second, second_sems, angle, tile)
    first_out[...] = first_sum[pl.ds(CHUNK, 8), :]
    second_sum[...] = finish_second(second, first_sum, landed_second, tile)
    third = start_third(second_sum, gathered, third_sems, angle, tile)
    gathered[angle] = second_sum[...]
    for copy in third + edges:
        copy.wait()


def rims_kernel(grad, parts, from_left, from_right, first_out, landed_first, edge_sems, first_sems):
    angle, tile = place()
    meet(angle_peers(angle, tile) + list(neighbours(angle, tile)))
    edges = start_edges(grad, from_left, from_right, edge_sems, angle, tile)
    first = start_first(parts, landed_first, first_sems, angle, tile)
    first_out[...] = finish_first(first, parts, landed_first, angle)
    for copy in edges:
        copy.wait()


def slabs_kernel(slabs, first_sum, gathered, second_out, landed_second, slab_sems, second_sems):
    angle, tile = place()
    meet(tile_peers(angle, tile))
    copies = []
    for step in range(1, TILES):
        owner = (tile + step) % TILES
        copies.append(send(slabs.at[owner], gathered.at[tile], slab_sems, step, (angle, owner)))
    second = start_second(first_sum, landed_second, second_sems, angle, tile)
    gathered[tile] = slabs[tile]
    second_out[...] = finish_second(second, first_sum, landed_second, tile)
    for copy in copies:
        copy.wait()


def rows_kernel(rows, second_sum, every, gathered, sems, third_sems):
    angle, tile = place()
    chip, core = angle // 2, angle % 2
    up, down, over = (chip + 1) % 4, (chip + 3) % 4, (chip + 2) % 4
    upper, lower, across = 2 * up + core, 2 * down + core, 2 * over + core
    sibling = 2 * chip + 1 - core
    meet(angle_peers(angle, tile))
    to_up = send(rows, every.at[angle], sems, 0, (upper, tile))
    to_down = send(rows, every.at[angle], sems, 1, (lower, tile))
    to_side = send(rows, every.at[angle], sems, 2, (sibling, tile))
    third = start_third(second_sum, gathered, third_sems, angle, tile)
    gathered[angle] = second_sum[...]
    every[angle] = rows[...]
    first_half, last_half = pl.ds(0, ZS // 2), pl.ds(ZS // 2, ZS // 2)
    to_up.wait_recv()
    on_up = send(every.at[lower, first_half], every.at[lower, first_half], sems, 3, (upper, tile))
    side_low = send(every.at[lower], every.at[lower], sems, 4, (sibling, tile))
    to_down.wait_recv()
    on_down = send(every.at[upper, last_half], every.at[upper, last_half], sems, 5, (lower, tile))
    side_up = send(every.at[upper], every.at[upper], sems, 6, (sibling, tile))
    on_up.wait_recv()
    side_first = send(every.at[across, first_half], every.at[across, first_half], sems, 7, (sibling, tile))
    on_down.wait_recv()
    side_last = send(every.at[across, last_half], every.at[across, last_half], sems, 8, (sibling, tile))
    for copy in (to_side, side_low, side_up, side_first, side_last):
        copy.wait()
    for copy in (to_up, to_down, on_up, on_down):
        copy.wait_send()
    for copy in third:
        copy.wait()


def gradients(counts, pos_z, pos_x, ext, probe, data, right_f, left_f, left_b, right_b, grad, parts, probe_acc):
    count = counts[0, 0]
    grad[...] = jnp.zeros_like(grad)
    probe_acc[...] = jnp.zeros_like(probe_acc)

    def pair(index, carry):
        probe_real, probe_imag = probe[0], probe[1]
        rows, windows, spots = [], [], []
        for offset in range(2):
            slot = 2 * index + offset
            start_z, start_x = pos_z[0, 0, slot], pos_x[0, 0, slot]
            back = lax.rem(WIDE - start_x, WIDE)
            here = pl.ds(start_z, PS)
            real, imag = (
                pltpu.roll(jnp.concatenate([ext[0, part, here, :], ext[1, part, here, :]], axis=1), back, 1)[:, :PS]
                for part in range(2)
            )
            windows.append((real, imag))
            spots.append((slot, start_z, start_x))
            wave = times((probe_real, probe_imag), (real, imag))
            rows.append(jnp.concatenate(wave, axis=1))
        half_way = dot_right(jnp.concatenate(rows, axis=0), right_f[...])
        stacked = jnp.concatenate(
            [
                jnp.concatenate([half_way[s * PS : (s + 1) * PS, :PS], half_way[s * PS : (s + 1) * PS, PS:]], axis=0)
                for s in range(2)
            ],
            axis=1,
        )
        far = dot_left(left_f[...], stacked)
        weighted = []
        for s in range(2):
            slot = spots[s][0]
            far_real, far_imag = far[:PS, s * PS : (s + 1) * PS], far[PS:, s * PS : (s + 1) * PS]
            live = jnp.where(slot < count, 1.0, 0.0).astype(F32)
            misfit = (far_real * far_real + far_imag * far_imag - data[slot]) * live
            weighted.append(jnp.concatenate([misfit * far_real, misfit * far_imag], axis=0))
        half_back = dot_left(left_b[...], jnp.concatenate(weighted, axis=1))
        stacked = jnp.concatenate(
            [
                jnp.concatenate([half_back[:PS, s * PS : (s + 1) * PS], half_back[PS:, s * PS : (s + 1) * PS]], axis=1)
                for s in range(2)
            ],
            axis=0,
        )
        chi = dot_right(stacked, right_b[...])
        zeros = jnp.zeros((PS, PS), F32)
        for s in range(2):
            slot, start_z, start_x = spots[s]
            chi_real, chi_imag = chi[s * PS : (s + 1) * PS, :PS], chi[s * PS : (s + 1) * PS, PS:]
            real, imag = windows[s]
            probe_acc[pl.ds(0, PS), :] += real * chi_real + imag * chi_imag
            probe_acc[pl.ds(PS, PS), :] += real * chi_imag - imag * chi_real
            grad_real = probe_real * chi_real + probe_imag * chi_imag
            grad_imag = probe_real * chi_imag - probe_imag * chi_real
            for part, value in ((0, grad_real), (1, grad_imag)):
                moved = pltpu.roll(jnp.concatenate([value, zeros], axis=1), start_x, 1)
                here = pl.ds(start_z, PS)
                grad[0, part, here, :] += moved[:, :TW]
                grad[1, part, here, :] += moved[:, TW:]
        return carry

    lax.fori_loop(0, (count + 1) // 2, pair, 0)
    for chunk in range(ANG):
        parts[chunk, pl.ds(0, CHUNK), :] = probe_acc[pl.ds(chunk * CHUNK, CHUNK), :]


def scalars_rows(counts, shears):
    angle = lax.axis_index("angle")
    row, lane = sublanes((8, TW)), lanes((8, TW))
    count = jnp.where((row == 0) & (lane == 0), counts[0, 0].astype(F32), 0.0)
    return jnp.where((row == 1) & (lane == angle), shears[0], count)


def first_kernel(
    counts, pos_z, pos_x, shears, psi, target, from_left, from_right, probe, data,
    right_f, left_f, left_b, right_b, ext, ext_target, grad, parts, probe_acc,
):
    tile = lax.axis_index("tile")
    low = lanes((ROWS, TW)) < HALF
    for index, (own, wide) in enumerate(((psi, ext), (target, ext_target))):
        before = jnp.where(tile > 0, from_left[index], 0.0)
        after = jnp.where(tile < TILES - 1, from_right[index], 0.0)
        real, imag = pltpu.roll(own[0], HALF, 1), pltpu.roll(own[1], HALF, 1)
        wide[0, 0] = jnp.where(low, before, real)
        wide[0, 1] = jnp.where(low, pltpu.roll(before, HALF, 1), imag)
        wide[1, 0] = jnp.where(low, real, pltpu.roll(after, HALF, 1))
        wide[1, 1] = jnp.where(low, imag, after)
    extra = scalars_rows(counts, shears)
    for chunk in range(ANG):
        parts[chunk, pl.ds(CHUNK, 8), :] = extra
    gradients(counts, pos_z, pos_x, ext, probe, data, right_f, left_f, left_b, right_b, grad, parts, probe_acc)


def second_kernel(
    counts, pos_z, pos_x, ext0, ext_target, grad0, from_left, from_right, probe0, gathered, data,
    right_f, left_f, left_b, right_b, ext, grad, parts, probe, probe_acc,
):
    tile = lax.axis_index("tile")
    low = lanes((ROWS, TW)) < HALF
    inner, outer = tile > 0, tile < TILES - 1
    for part in range(2):
        for side, landed, inside in ((0, from_left, inner), (1, from_right, outer)):
            total = grad0[side, part] + jnp.where(inside, landed[part], 0.0)
            old = ext0[side, part]
            new = old - ALPHA * (total + RHO * (old - ext_target[side, part]))
            keep = jnp.logical_or(inside, jnp.logical_not(low) if side == 0 else low)
            ext[side, part] = jnp.where(keep, new, 0.0)
    number = gathered[0, pl.ds(CHUNK, 1), pl.ds(0, 1)]
    for chunk in range(ANG):
        part, start = divmod(chunk * CHUNK, PS)
        step = PROBE_STEP * gathered[chunk, pl.ds(0, CHUNK), :] / number
        probe[part, pl.ds(start, CHUNK), :] = probe0[part, pl.ds(start, CHUNK), :] - step
        parts[chunk, pl.ds(CHUNK, 8), :] = gathered[chunk, pl.ds(CHUNK, 8), :]
    gradients(counts, pos_z, pos_x, ext, probe, data, right_f, left_f, left_b, right_b, grad, parts, probe_acc)


def update_kernel(ext, target, grad, from_left, from_right, psi_new, slabs):
    tile = lax.axis_index("tile")
    low = lanes((ROWS, TW)) < HALF
    for part in range(2):
        before = jnp.where(tile > 0, from_left[part], 0.0)
        after = jnp.where(tile < TILES - 1, from_right[part], 0.0)
        left = grad[0, part] + before
        right = grad[1, part] + after
        old = jnp.where(low, pltpu.roll(ext[0, part], HALF, 1), pltpu.roll(ext[1, part], HALF, 1))
        total = jnp.where(low, pltpu.roll(left, HALF, 1), pltpu.roll(right, HALF, 1))
        goal = target[part]
        new = old - ALPHA * (total + RHO * (old - goal))
        psi_new[part] = new
        gap = goal - new
        for slab in range(TILES):
            slabs[slab, part] = gap[slab * ZS : (slab + 1) * ZS]


def spectrum_kernel(slabs, turns, right_f, rows, work):
    items = [(slabs[tile, 0], slabs[tile, 1]) for tile in range(TILES)]
    work[...] = jnp.zeros_like(work)
    for order, item in enumerate(sixteen(items, -1)):
        turn = (turns[0, pl.ds(order, 1), :], turns[1, pl.ds(order, 1), :])
        real, imag = times(item, turn)
        work[pl.ds(16 * order, ZS), pl.ds(0, TW)] = real
        work[pl.ds(16 * order, ZS), pl.ds(TW, TW)] = imag
    result = dot_right(work[...], right_f[...])
    for order in range(TILES):
        rows[:, order, :] = result[16 * order : 16 * order + ZS]


def flip8(value):
    row = sublanes(value.shape)
    value = pltpu.roll(value, 4, 0)
    value = jnp.where((row & 2) == 0, pltpu.roll(value, 6, 0), pltpu.roll(value, 2, 0))
    return jnp.where((row & 1) == 0, pltpu.roll(value, 7, 0), pltpu.roll(value, 1, 0))


def image_kernel(
    rows, shear_rows, turns, right_b, probe0, gathered, counted, image, probe_new,
    bases, cosines, sines, turned, spread, middle,
):
    @pl.when(pl.program_id(0) == 0)
    def _():
        number = counted[0, pl.ds(CHUNK, 1), pl.ds(0, 1)]
        for chunk in range(ANG):
            part, start = divmod(chunk * CHUNK, PS)
            step = PROBE_STEP * gathered[chunk, pl.ds(0, CHUNK), :] / number
            probe_new[part, pl.ds(start, CHUNK), :] = probe0[part, pl.ds(start, CHUNK), :] - step
        frequency = sublanes((TILES, TW)) + TILES * lanes((TILES, TW))
        signed = jnp.where(frequency < H // 2, frequency, frequency - H).astype(F32)
        centre = (YB * lax.axis_index("angle") - ANG * YB // 2).astype(F32) + (YB - 1) / 2.0
        row = sublanes((8, TW))

        for angle in range(ANG):
            turn = signed * (1.0 / H) * shear_rows[pl.ds(1, 1), pl.ds(angle, 1)]
            whole = centre * turn
            whole = 2.0 * math.pi * (whole - jnp.round(whole))
            half = math.pi * turn
            bases[angle, 0], bases[angle, 1] = jnp.cos(whole), jnp.sin(whole)
            power = (jnp.cos(half), jnp.sin(half))
            for level in range(5):
                bases[angle, 2 + 2 * level], bases[angle, 3 + 2 * level] = power
                power = times(power, power)

        def fill(angle, carry):
            for order in range(TILES):
                line = [
                    tuple(
                        jnp.broadcast_to(bases[angle, 2 + 2 * level + part, pl.ds(order, 1), :], (8, TW))
                        for part in range(2)
                    )
                    for level in range(5)
                ]
                now = line[0]
                for level in range(3):
                    ahead = times(now, line[1 + level])
                    chosen = (row & (1 << level)) != 0
                    now = tuple(jnp.where(chosen, new, old) for new, old in zip(ahead, now))
                later = times(now, line[4])
                cosines[angle, order, pl.ds(0, 8), :], sines[angle, order, pl.ds(0, 8), :] = now
                cosines[angle, order, pl.ds(8, 8), :], sines[angle, order, pl.ds(8, 8), :] = later
            return carry

        lax.fori_loop(0, ANG, fill, 0)

    for angle in range(ANG):
        value = (rows[angle, 0, :, pl.ds(0, TW)], rows[angle, 0, :, pl.ds(TW, TW)])
        turned[angle, 0], turned[angle, 1] = times(value, (bases[angle, 0], bases[angle, 1]))

    for order in range(TILES):
        sums = None
        for angle in range(ANG):
            real = jnp.broadcast_to(turned[angle, 0, pl.ds(order, 1), :], (16, TW))
            imag = jnp.broadcast_to(turned[angle, 1, pl.ds(order, 1), :], (16, TW))
            cosine, sine = cosines[angle, order], sines[angle, order]
            terms = (real * cosine, imag * sine, real * sine, imag * cosine)
            sums = terms if sums is None else tuple(s + t for s, t in zip(sums, terms))
        rc, isn, rs, ic = sums
        above = (rc - isn, rs + ic)
        below = (rc + isn, ic - rs)
        for part in range(2):
            back = jnp.concatenate([flip8(below[part][8:]), flip8(below[part][:8])], axis=0)
            value = jnp.concatenate([back, above[part]], axis=0)
            high, low = split(value)
            here = pl.ds(order * YB, YB)
            spread[here, pl.ds(part * TW, TW)] = high
            spread[here, pl.ds((2 + part) * TW, TW)] = low
            spread[here, pl.ds((4 + part) * TW, TW)] = high

    middle[...] = jnp.dot(spread[...], right_b[...], preferred_element_type=F32)

    def finish(group, carry):
        items = []
        for order in range(TILES):
            here = pl.ds(pl.multiple_of(order * YB + 16 * group, 16), 16)
            value = (middle[here, pl.ds(0, TW)], middle[here, pl.ds(TW, TW)])
            turn = (turns[0, pl.ds(order, 1), :], turns[1, pl.ds(order, 1), :])
            items.append(times(value, turn))
        for tile, item in enumerate(sixteen(items, 1)):
            for part in range(2):
                image[part, 0, pl.ds(pl.multiple_of(16 * group, 16), 16), pl.ds(tile * TW, TW)] = item[part].astype(BF16)
        return carry

    lax.fori_loop(0, YB // 16, finish, 0)


def arr(*shape):
    return jax.ShapeDtypeStruct(shape, F32)


def dma(*shape):
    return pltpu.SemaphoreType.DMA(shape)


def remote(kernel, outs, scratch, ident):
    return pl.pallas_call(
        kernel,
        out_shape=outs,
        in_specs=[VMEM, VMEM],
        out_specs=[VMEM] * len(outs),
        scratch_shapes=scratch,
        compiler_params=pltpu.CompilerParams(collective_id=ident, has_side_effects=True, vmem_limit_bytes=VLIMIT),
    )


def local(kernel, outs, specs, scratch):
    return pl.pallas_call(
        kernel,
        out_shape=outs,
        in_specs=specs,
        out_specs=[VMEM] * len(outs),
        scratch_shapes=scratch,
        compiler_params=pltpu.CompilerParams(vmem_limit_bytes=VLIMIT),
    )


def image_call(rows, shear_rows, turns, table, probe, gathered, counted):
    full = lambda *shape: pl.BlockSpec(shape, lambda z: (0,) * len(shape))
    return pl.pallas_call(
        image_kernel,
        grid=(ZS,),
        out_shape=[jax.ShapeDtypeStruct((2, ZS, YB, H), BF16), arr(2, PS, PS)],
        in_specs=[
            pl.BlockSpec((ANG, 1, TILES, WIDE), lambda z: (0, z, 0, 0)),
            full(8, TW),
            full(2, TILES, TW),
            full(3 * WIDE, WIDE),
            full(2, PS, PS),
            full(ANG, CROWS, TW),
            full(ANG, CROWS, TW),
        ],
        out_specs=[pl.BlockSpec((2, 1, YB, H), lambda z: (0, z, 0, 0)), full(2, PS, PS)],
        scratch_shapes=[
            pltpu.VMEM((ANG, 12, TILES, TW), F32),
            pltpu.VMEM((ANG, TILES, 16, TW), F32),
            pltpu.VMEM((ANG, TILES, 16, TW), F32),
            pltpu.VMEM((ANG, 2, TILES, TW), F32),
            pltpu.VMEM((TILES * YB, 3 * WIDE), BF16),
            pltpu.VMEM((TILES * YB, WIDE), F32),
        ],
        compiler_params=pltpu.CompilerParams(vmem_limit_bytes=VLIMIT),
    )(rows, shear_rows, turns, table, probe, gathered, counted)


def shards(psi, target, probe, data, pos_z, pos_x, counts, shears):
    psi, target = psi.reshape(2, ROWS, TW), target.reshape(2, ROWS, TW)
    data = data.reshape(CAP, PS, PS)
    unit = dft_block(PS, 1.0 / math.sqrt(PS))
    tables = [
        jnp.asarray(t)
        for t in (right_table(unit), left_table(unit.T), left_table(unit), right_table(unit.T))
    ]
    wide, edge = arr(2, 2, ROWS, TW), arr(2, ROWS, TW)
    small, chunks = arr(8, TW), arr(ANG, CROWS, TW)
    one = lambda *shape: pltpu.VMEM(shape, F32)
    accumulate = [one(2 * PS, PS)]

    from_left, from_right = remote(
        halo_kernel, [edge, edge], [one(2, ROWS, TW), one(2, ROWS, TW), dma(2, 2)], 0
    )(psi, target)
    ext, ext_target, grad, parts = local(
        first_kernel, [wide, wide, wide, chunks], [SMEM] * 4 + [VMEM] * 10, accumulate
    )(counts, pos_z, pos_x, shears, psi, target, from_left, from_right, probe, data, *tables)
    from_left, from_right, shear_rows, counted = remote(
        exchange_kernel,
        [edge, edge, small, chunks],
        [
            one(ANG, CROWS, TW), one(CROWS, TW), one(TILES, CROWS, TW), one(CROWS, TW),
            dma(2, 2), dma(2, ANG), dma(2, TILES), dma(2, ANG),
        ],
        1,
    )(grad, parts)
    ext, grad, parts, probe = local(
        second_kernel, [wide, wide, chunks, arr(2, PS, PS)], [SMEM] * 3 + [VMEM] * 12, accumulate
    )(counts, pos_z, pos_x, ext, ext_target, grad, from_left, from_right, probe, counted, data, *tables)
    from_left, from_right, first_sum = remote(
        rims_kernel,
        [edge, edge, arr(CROWS, TW)],
        [one(ANG, CROWS, TW), dma(2, 2), dma(2, ANG)],
        2,
    )(grad, parts)
    psi_new, slabs = local(update_kernel, [edge, arr(TILES, 2, ZS, TW)], [VMEM] * 5, [])(
        ext, target, grad, from_left, from_right
    )
    slabs, second_sum = remote(
        slabs_kernel,
        [arr(TILES, 2, ZS, TW), arr(CROWS, TW)],
        [one(TILES, CROWS, TW), dma(2, TILES), dma(2, TILES)],
        3,
    )(slabs, first_sum)
    (rows,) = local(spectrum_kernel, [arr(ZS, TILES, WIDE)], [VMEM] * 3, [one(WIDE, WIDE)])(
        slabs, jnp.asarray(turn_table(-1)), jnp.asarray(right_table(dft_block(TW, 1.0)))
    )
    every, gathered = remote(
        rows_kernel, [arr(ANG, ZS, TILES, WIDE), chunks], [dma(2, 9), dma(2, ANG)], 4
    )(rows, second_sum)
    inverse = dft_block(TW, 1.0 / (H * ANG)).T
    image, probe_new = image_call(
        every, shear_rows, jnp.asarray(turn_table(1)), jnp.asarray(right_table(inverse)), probe, gathered, counted
    )
    return psi_new.reshape(2, 1, ROWS, TW), probe_new, image


def solution(mesh):
    in_specs = (
        P(None, "angle", None, "tile"),
        P(None, "angle", None, "tile"),
        P(),
        P("angle", "tile", None, None, None),
        P("angle", "tile", None),
        P("angle", "tile", None),
        P("angle", "tile"),
        P("angle"),
    )
    out_specs = (P(None, "angle", None, "tile"), P(), P(None, "tile", "angle", None))
    return jax.shard_map(shards, mesh=mesh, in_specs=in_specs, out_specs=out_specs, check_vma=False)
```

time: 922 us -> 123 us (0.13); the launches traced: 911 us -> 123 us
  matrix products: 346 us -> 0 us
  waiting for transfers between devices: 295 us -> 0 us
  local copies, waits for them, and re-layouts: 127 us -> 0 us
  Pallas kernels: 0 us -> 121 us
  blocking collectives: 84.3 us -> 0 us
  starting transfers between devices: 26.6 us -> 0 us
  other arithmetic: 14.5 us -> 0 us
  between operations: 16.1 us -> 1.96 us
    dot_general x56 -> x0, matrix products: 346 us -> none  [the longest x13 86.1 us: twin_einsum(): jnp.einsum(pattern, left_imag, right_real, precision=HIGHEST)]
    psum x2 -> x0, waiting for transfers between devices: 274 us -> none  [shards(): lax.psum((probe_part, local_count), ('angle', 'tile'))]
    pallas_call x0 -> x10, Pallas kernels: none -> 121 us  [the longest x1 28.8 us: shards(): remote(exchange_kernel, [edge, edge, small, chunks], [one(ANG, CROWS, TW)...]
    gather x96 -> x0, local copies, waits for them, and re-layouts: 79.4 us -> none
    psum x1 -> x0, blocking collectives: 69.6 us -> none  [shards(): lax.psum((probe_part, local_count), ('angle', 'tile'))]
    ppermute x8 -> x0, starting transfers between devices: 19.7 us -> none  [the longest x4 14.5 us: extended_2(): lax.ppermute(lax.slice_in_dim(block, block.shape[dim] - width, None, axis...]
    reshape x2 -> x0, local copies, waits for them, and re-layouts: 18.9 us -> none  [the longest x1 9.45 us: inverse_rows(): shaped_real = values_real.reshape(leading + (outer, inner))]
    unnamed x1 -> x0, blocking collectives: 14.7 us -> none
  transfers between devices with their start and end apart: 12 -> 0, of which waited for: 7 -> 0; matrix products, arithmetic and copies ran while one was open for 2% -> 0% of each run, Pallas kernels for 0% -> 0%
where the time goes in v1:
time: 123 us
  Pallas kernels  121 us (98%)
  between operations  1.96 us (2%)
    pallas_call x1, Pallas kernels, shards(): remote(exchange_kernel, [edge, edge, small, chunks], [one(ANG, CROWS, TW)...  28.8 us
    pallas_call x1, Pallas kernels, shards(): remote(rows_kernel, [arr(ANG, ZS, TILES, WIDE), chunks], [dma(2, 9), dma(...  18.4 us
    pallas_call x1, Pallas kernels, shards(): remote(rims_kernel, [edge, edge, arr(CROWS, TW)], [one(ANG, CROWS, TW), d...  16.8 us
    pallas_call x1, Pallas kernels, shards(): remote(halo_kernel, [edge, edge], [one(2, ROWS, TW), one(2, ROWS, TW), dm...  12.9 us
    pallas_call x1, Pallas kernels, image_call(): pl.pallas_call(image_kernel, grid=(ZS,), out_shape=[jax.ShapeDtypeStruct(...  12.8 us
    pallas_call x1, Pallas kernels, shards(): remote(slabs_kernel, [arr(TILES, 2, ZS, TW), arr(CROWS, TW)], [one(TILES,...  10.8 us
    pallas_call x1, Pallas kernels, shards(): local(second_kernel, [wide, wide, chunks, arr(2, PS, PS)], [SMEM] * 3 + [...  7.86 us
    pallas_call x1, Pallas kernels, shards(): local(first_kernel, [wide, wide, wide, chunks], [SMEM] * 4 + [VMEM] * 10,...  7.77 us

profile of v1, /device:TPU:1, one launch (start us, length us, event | category | flops | bytes accessed | tf_op | source)
XLA Modules:
  0.0 122.5 jit_solution(12250787699581187559)
XLA Ops:
  1.9 12.9 %shard_map.175 = (f32[2,160,128]{2,1,0:T(8,128)}, f32[2,160,128]{2,1,0:T(8,128)}) custom-call(f32[2,160,128]{2,1,0:T(8,128)} %bitcast.11, f32[2,160,128]{2,1,0:T(8,128)} %bitcast.8), custom_call_target="tpu_custom_call" | custom-call | tf_op jit(solution)/shard_map/pallas_call | solution.py:614
  14.8 7.8 %shard_map.176 = (f32[2,2,160,128]{3,2,1,0:T(8,128)}, f32[2,2,160,128]{3,2,1,0:T(8,128)}, f32[2,2,160,128]{3,2,1,0:T(8,128)}, f32[8,40,128]{2,1,0:T(8,128)}) custom-call(s32[1,1]{1,0:T(1,128)S(6)} %copy.20.counts, s32[1,1,16]{2,1,0:T(1,128)} %pos_z.3, s32[1,1,16]{2,1,0:T(1,128)} %pos_x.3, f32[1]{0:T(128)S(6)} %copy.21.shears, f32[2,160,128]{2,1,0:T(8,128)} %bitcast.12, ...), custom_call_target="tpu_custom_call" | custom-call | tf_op jit(solution)/shard_map/pallas_call | solution.py:617
  22.6 28.8 %shard_map.177 = (f32[2,160,128]{2,1,0:T(8,128)}, f32[2,160,128]{2,1,0:T(8,128)}, f32[8,128]{1,0:T(8,128)}, f32[8,40,128]{2,1,0:T(8,128)}) custom-call(f32[2,2,160,128]{3,2,1,0:T(8,128)} %get-tuple-element.32.grad.grad0, f32[8,40,128]{2,1,0:T(8,128)} %get-tuple-element.33.parts), custom_call_target="tpu_custom_call" | custom-call | tf_op jit(solution)/shard_map/pallas_call | solution.py:620
  51.5 7.9 %shard_map.178 = (f32[2,2,160,128]{3,2,1,0:T(8,128)}, f32[2,2,160,128]{3,2,1,0:T(8,128)}, f32[8,40,128]{2,1,0:T(8,128)}, f32[2,128,128]{2,1,0:T(8,128)}) custom-call(s32[1,1]{1,0:T(1,128)S(6)} %copy.20.counts, s32[1,1,16]{2,1,0:T(1,128)} %pos_z.3, s32[1,1,16]{2,1,0:T(1,128)} %pos_x.3, f32[2,2,160,128]{3,2,1,0:T(8,128)} %get-tuple-element.30.ext0, ...), custom_call_target="tpu_custom_call" | custom-call | tf_op jit(solution)/shard_map/pallas_call | solution.py:629
  59.3 16.8 %shard_map.179 = (f32[2,160,128]{2,1,0:T(8,128)}, f32[2,160,128]{2,1,0:T(8,128)}, f32[40,128]{1,0:T(8,128)}) custom-call(f32[2,2,160,128]{3,2,1,0:T(8,128)} %get-tuple-element.38.grad, f32[8,40,128]{2,1,0:T(8,128)} %get-tuple-element.39.parts), custom_call_target="tpu_custom_call" | custom-call | tf_op jit(solution)/shard_map/pallas_call | solution.py:632
  76.1 2.3 %shard_map.180 = (f32[2,160,128]{2,1,0:T(8,128)}, f32[16,2,10,128]{3,2,1,0:T(8,128)}) custom-call(f32[2,2,160,128]{3,2,1,0:T(8,128)} %get-tuple-element.37.ext, f32[2,160,128]{2,1,0:T(8,128)} %bitcast.10, f32[2,2,160,128]{3,2,1,0:T(8,128)} %get-tuple-element.38.grad, f32[2,160,128]{2,1,0:T(8,128)} %get-tuple-element.40.from_left, ...), custom_call_target="tpu_custom_call" | custom-call | tf_op jit(solution)/shard_map/pallas_call | solution.py:638
  78.4 10.8 %shard_map.181 = (f32[16,2,10,128]{3,2,1,0:T(8,128)}, f32[40,128]{1,0:T(8,128)}) custom-call(f32[16,2,10,128]{3,2,1,0:T(8,128)} %get-tuple-element.43.slabs, f32[40,128]{1,0:T(8,128)} %get-tuple-element.44.first_sum), custom_call_target="tpu_custom_call" | custom-call | tf_op jit(solution)/shard_map/pallas_call | solution.py:641
  89.2 2.1 %shard_map.182.rows = f32[10,16,256]{2,1,0:T(8,128)} custom-call(f32[16,2,10,128]{3,2,1,0:T(8,128)} %get-tuple-element.45.slabs, f32[2,16,128]{2,1,0:T(8,128)} %constant.20.clone.turns, bf16[768,256]{1,0:T(8,128)(2,1)} %constant.21.clone.right_f), custom_call_target="tpu_custom_call" | custom-call | tf_op jit(solution)/shard_map/pallas_call | solution.py:647
  91.3 18.4 %shard_map.183 = (f32[8,10,16,256]{3,2,1,0:T(8,128)}, f32[8,40,128]{2,1,0:T(8,128)}) custom-call(f32[10,16,256]{2,1,0:T(8,128)} %shard_map.182.rows, f32[40,128]{1,0:T(8,128)} %get-tuple-element.46.second_sum), custom_call_target="tpu_custom_call" | custom-call | tf_op jit(solution)/shard_map/pallas_call | solution.py:650
  109.7 12.8 %shard_map.184 = (bf16[2,10,32,2048]{3,2,1,0:T(8,128)(2,1)}, f32[2,128,128]{2,1,0:T(8,128)}) custom-call(f32[8,10,16,256]{3,2,1,0:T(8,128)} %get-tuple-element.47.rows, f32[8,128]{1,0:T(8,128)} %get-tuple-element.48.shear_rows, f32[2,16,128]{2,1,0:T(8,128)} %constant.22.clone.turns, bf16[768,256]{1,0:T(8,128)(2,1)} %constant.23.clone.right_b, ...), custom_call_target="tpu_custom_call" | custom-call | tf_op jit(solution)/shard_map/pallas_call | solution.py:575

commit v2 on v1

v2 whole, which is shorter than its diff:
```python
import functools
import math

import jax
import jax.numpy as jnp
import numpy as np
from jax import lax
from jax.experimental import pallas as pl
from jax.experimental.pallas import tpu as pltpu
from jax.sharding import PartitionSpec as P

ITERS = 2
ALPHA = 0.004
RHO = 5.0
PROBE_STEP = 0.02

ANG = 8
TILES = 16
PS = 128
TW = 128
ROWS = 160
CAP = 16
HALF = 64
WIDE = 256
ZS = ROWS // TILES
YB = 32
H = 2048
CHUNK = 2 * PS // ANG
GROUP = 4

F32 = jnp.float32
BF16 = jnp.bfloat16
MESH = pl.DeviceIdType.MESH
VMEM = pl.BlockSpec(memory_space=pltpu.VMEM)
SMEM = pl.BlockSpec(memory_space=pltpu.SMEM)
HBM = pl.BlockSpec(memory_space=pltpu.HBM)
VLIMIT = 20 * 1024 * 1024


def dft_block(length, scale):
    index = np.arange(length)
    turns = (index[:, None] * index[None, :]) % length
    angle = -2.0 * math.pi * turns / length
    real, imag = np.cos(angle) * scale, np.sin(angle) * scale
    return np.block([[real, imag], [-imag, real]])


def split_const(matrix):
    high = matrix.astype(BF16)
    low = (matrix - high.astype(np.float64)).astype(BF16)
    return high, low


def right_table(matrix):
    high, low = split_const(matrix)
    return np.concatenate([high, high, low], axis=0)


def left_table(matrix):
    high, low = split_const(matrix)
    return np.concatenate([high, high, low], axis=1)


def turn_table(orient):
    angle = orient * 2.0 * math.pi * np.arange(TILES)[:, None] * np.arange(TW)[None, :] / H
    return np.stack([np.cos(angle), np.sin(angle)]).astype(np.float32)


def split(value):
    high = value.astype(BF16)
    low = (value - high.astype(F32)).astype(BF16)
    return high, low


def dot_right(value, table):
    high, low = split(value)
    return jnp.dot(jnp.concatenate([high, low, high], axis=1), table, preferred_element_type=F32)


def dot_left(table, value):
    high, low = split(value)
    return jnp.dot(table, jnp.concatenate([high, low, high], axis=0), preferred_element_type=F32)


def times(left, right):
    return left[0] * right[0] - left[1] * right[1], left[0] * right[1] + left[1] * right[0]


def four(items, orient):
    (ar, ai), (br, bi), (cr, ci), (dr, di) = items
    sr, si, ur, ui = ar + cr, ai + ci, ar - cr, ai - ci
    pr, pi, qr, qi = br + dr, bi + di, br - dr, bi - di
    first = (sr + pr, si + pi)
    third = (sr - pr, si - pi)
    plus = (ur - qi, ui + qr)
    minus = (ur + qi, ui - qr)
    return [first, plus, third, minus] if orient > 0 else [first, minus, third, plus]


def sixteen(items, orient):
    columns = []
    for fine in range(4):
        partial = four([items[4 * coarse + fine] for coarse in range(4)], orient)
        for order in range(1, 4):
            step = fine * order
            if step:
                angle = orient * 2.0 * math.pi * step / 16
                partial[order] = times(partial[order], (math.cos(angle), math.sin(angle)))
        columns.append(partial)
    result = [None] * 16
    for low in range(4):
        finished = four([columns[fine][low] for fine in range(4)], orient)
        for high in range(4):
            result[low + 4 * high] = finished[high]
    return result


def lanes(shape):
    return lax.broadcasted_iota(jnp.int32, shape, len(shape) - 1)


def sublanes(shape):
    return lax.broadcasted_iota(jnp.int32, shape, len(shape) - 2)


def place():
    return lax.axis_index("angle"), lax.axis_index("tile")


def meet(peers):
    barrier = pltpu.get_barrier_semaphore()
    for peer in peers:
        pl.semaphore_signal(barrier, inc=1, device_id=peer, device_id_type=MESH)
    pl.semaphore_wait(barrier, len(peers))


def send(source, target, sems, slot, peer):
    copy = pltpu.make_async_remote_copy(
        src_ref=source,
        dst_ref=target,
        send_sem=sems.at[0, slot],
        recv_sem=sems.at[1, slot],
        device_id=peer,
        device_id_type=MESH,
    )
    copy.start()
    return copy


def angle_peers(angle, tile):
    return [((angle + step) % ANG, tile) for step in range(1, ANG)]


def tile_peers(angle, tile):
    return [(angle, (tile + step) % TILES) for step in range(1, TILES)]


def neighbours(angle, tile):
    return (angle, (tile + TILES - 1) % TILES), (angle, (tile + 1) % TILES)


def start_edges(packs, from_left, from_right, sems, angle, tile):
    left, right = neighbours(angle, tile)
    return [
        send(packs.at[0], from_right, sems, 0, left),
        send(packs.at[1], from_left, sems, 1, right),
    ]


def start_first(parts, landed, sems, angle, tile):
    return [
        send(parts.at[(angle + step) % ANG], landed.at[step], sems, step, ((angle + step) % ANG, tile))
        for step in range(1, ANG)
    ]


def finish_first(copies, parts, landed, angle):
    for copy in copies:
        copy.wait()
    total = parts[angle]
    for step in range(1, ANG):
        total = total + landed[step]
    return total


def start_second(source, landed, sems, angle, tile):
    return [
        send(source, landed.at[tile], sems, step, (angle, (tile + step) % TILES))
        for step in range(1, TILES)
    ]


def finish_second(copies, source, landed, tile):
    landed[tile] = source[...]
    for copy in copies:
        copy.wait()
    total = landed[0]
    for index in range(1, TILES):
        total = total + landed[index]
    return total


def start_third(source, gathered, sems, angle, tile):
    return [
        send(source, gathered.at[angle], sems, step, ((angle + step) % ANG, tile))
        for step in range(1, ANG)
    ]


def packed_sides(real, imag):
    low = lanes((ROWS, TW)) < HALF
    return (
        jnp.where(low, real, pltpu.roll(imag, HALF, 1)),
        jnp.where(low, pltpu.roll(real, HALF, 1), imag),
    )


def widened(real, imag, before, after, tile):
    low = lanes((ROWS, TW)) < HALF
    before = jnp.where(tile > 0, before, 0.0)
    after = jnp.where(tile < TILES - 1, after, 0.0)
    real, imag = pltpu.roll(real, HALF, 1), pltpu.roll(imag, HALF, 1)
    return (
        (jnp.where(low, before, real), jnp.where(low, pltpu.roll(before, HALF, 1), imag)),
        (jnp.where(low, real, pltpu.roll(after, HALF, 1)), jnp.where(low, imag, after)),
    )


def halo_kernel(
    counts, shears, psi, target, probe, data, *refs,
):
    tables, refs = refs[:4], refs[4:]
    ext, own_target, packs, info, probe_here, data_here, *refs = refs
    tables_here, refs = refs[:4], refs[4:]
    own, sides, from_left, from_right, block, landed, edge_sems, info_sems, local_sems = refs
    angle, tile = place()
    fetches = [
        pltpu.make_async_copy(source, here, local_sems.at[index])
        for index, (source, here) in enumerate(
            zip((psi, target, probe, data) + tables, (own, own_target, probe_here, data_here) + tuple(tables_here))
        )
    ]
    for fetch in fetches:
        fetch.start()
    row, lane = sublanes((8, TW)), lanes((8, TW))
    count = jnp.where((row == 0) & (lane == 0), counts[0, 0].astype(F32), 0.0)
    block[...] = jnp.where((row == 1) & (lane == angle), shears[0], count)
    fetches[0].wait()
    for side, value in enumerate(packed_sides(own[0], own[1])):
        sides[side] = value
    meet(angle_peers(angle, tile) + list(neighbours(angle, tile)))
    edges = start_edges(sides, from_left, from_right, edge_sems, angle, tile)
    infos = [
        send(block, landed.at[step], info_sems, step, ((angle + step) % ANG, tile)) for step in range(1, ANG)
    ]
    fetches[1].wait()
    for side, value in enumerate(packed_sides(own_target[0], own_target[1])):
        packs[side] = value
    for fetch in fetches[2:]:
        fetch.wait()
    for copy in edges:
        copy.wait()
    for side, pair in enumerate(widened(own[0], own[1], from_left[...], from_right[...], tile)):
        for part in range(2):
            ext[side, part] = pair[part]
    for copy in infos:
        copy.wait()
    total = block[...]
    for step in range(1, ANG):
        total = total + landed[step]
    info[...] = total


def exchange_kernel(
    grad, parts, packs, info, ext0, own_target, probe0, ext, probe, info_all,
    from_left, from_right, goal_left, goal_right, landed_first, first_sum, landed_second, second_sum, gathered, landed_info,
    edge_sems, goal_sems, first_sems, second_sems, third_sems, info_sems,
):
    angle, tile = place()
    meet(angle_peers(angle, tile) + tile_peers(angle, tile))
    first = start_first(parts, landed_first, first_sems, angle, tile)
    edges = start_edges(grad, from_left, from_right, edge_sems, angle, tile)
    infos = start_second(info, landed_info, info_sems, angle, tile)
    goals = start_edges(packs, goal_left, goal_right, goal_sems, angle, tile)
    first_sum[...] = finish_first(first, parts, landed_first, angle)
    second = start_second(first_sum, landed_second, second_sems, angle, tile)
    for copy in edges + goals:
        copy.wait()
    low = lanes((ROWS, TW)) < HALF
    inner, outer = tile > 0, tile < TILES - 1
    goal = widened(own_target[0], own_target[1], goal_left[...], goal_right[...], tile)
    for side, landed, inside in ((0, from_left, inner), (1, from_right, outer)):
        for part in range(2):
            total = grad[side, part] + jnp.where(inside, landed[part], 0.0)
            old = ext0[side, part]
            new = old - ALPHA * (total + RHO * (old - goal[side][part]))
            keep = jnp.logical_or(inside, jnp.logical_not(low) if side == 0 else low)
            ext[side, part] = jnp.where(keep, new, 0.0)
    info_all[...] = finish_second(infos, info, landed_info, tile)
    second_sum[...] = finish_second(second, first_sum, landed_second, tile)
    third = start_third(second_sum, gathered, third_sems, angle, tile)
    gathered[angle] = second_sum[...]
    number = info_all[pl.ds(0, 1), pl.ds(0, 1)]
    for copy in third:
        copy.wait()
    for chunk in range(ANG):
        part, start = divmod(chunk * CHUNK, PS)
        here = pl.ds(start, CHUNK)
        probe[part, here, :] = probe0[part, here, :] - PROBE_STEP * gathered[chunk] / number


def tail_kernel(
    ext, own_target, grad, rims, parts, info, turns, right_f,
    psi_new, every, gathered, bases, cosines, sines,
    from_left, from_right, landed_first, first_sum, landed_second, second_sum, slabs, slabs_here, work, rows,
    edge_sems, first_sems, second_sems, third_sems, slab_sems, row_sems,
):
    angle, tile = place()
    meet(angle_peers(angle, tile) + tile_peers(angle, tile))
    edges = start_edges(rims, from_left, from_right, edge_sems, angle, tile)
    first = start_first(parts, landed_first, first_sems, angle, tile)
    low = lanes((ROWS, TW)) < HALF
    inner, outer = tile > 0, tile < TILES - 1
    for part in range(2):
        old, total = (
            jnp.where(low, pltpu.roll(wide[0, part], HALF, 1), pltpu.roll(wide[1, part], HALF, 1))
            for wide in (ext, grad)
        )
        psi_new[part] = old - ALPHA * (total + RHO * (old - own_target[part]))
    for copy in edges:
        copy.wait()
    for part in range(2):
        before = jnp.where(inner, from_left[...], 0.0)
        after = jnp.where(outer, from_right[...], 0.0)
        if part == 0:
            extra = jnp.where(low, before, pltpu.roll(after, HALF, 1))
        else:
            extra = jnp.where(low, pltpu.roll(before, HALF, 1), after)
        new = psi_new[part] - ALPHA * extra
        psi_new[part] = new
        gap = own_target[part] - new
        for slab in range(TILES):
            slabs[slab, part] = gap[slab * ZS : (slab + 1) * ZS]
    copies = []
    for step in range(1, TILES):
        owner = (tile + step) % TILES
        copies.append(send(slabs.at[owner], slabs_here.at[tile], slab_sems, step, (angle, owner)))
    slabs_here[tile] = slabs[tile]
    first_sum[...] = finish_first(first, parts, landed_first, angle)
    second = start_second(first_sum, landed_second, second_sems, angle, tile)
    for copy in copies:
        copy.wait()

    items = [(slabs_here[index, 0], slabs_here[index, 1]) for index in range(TILES)]
    work[...] = jnp.zeros_like(work)
    for order, item in enumerate(sixteen(items, -1)):
        turn = (turns[0, pl.ds(order, 1), :], turns[1, pl.ds(order, 1), :])
        real, imag = times(item, turn)
        work[pl.ds(16 * order, ZS), pl.ds(0, TW)] = real
        work[pl.ds(16 * order, ZS), pl.ds(TW, TW)] = imag
    result = dot_right(work[...], right_f[...])
    for order in range(TILES):
        rows[:, order, :] = result[16 * order : 16 * order + ZS]

    chip, core = angle // 2, angle % 2
    up, down, over = (chip + 1) % 4, (chip + 3) % 4, (chip + 2) % 4
    upper, lower, across = 2 * up + core, 2 * down + core, 2 * over + core
    above, below, beside = (upper, tile), (lower, tile), (2 * chip + 1 - core, tile)
    one, two = pl.ds(0, ZS // 2), pl.ds(ZS // 2, ZS // 2)
    up_one = send(rows.at[one], every.at[angle, one], row_sems, 0, above)
    down_two = send(rows.at[two], every.at[angle, two], row_sems, 1, below)
    up_two = send(rows.at[two], every.at[angle, two], row_sems, 2, above)
    down_one = send(rows.at[one], every.at[angle, one], row_sems, 3, below)
    side = send(rows, every.at[angle], row_sems, 4, beside)
    every[angle] = rows[...]
    second_sum[...] = finish_second(second, first_sum, landed_second, tile)
    third = start_third(second_sum, gathered, third_sems, angle, tile)
    gathered[angle] = second_sum[...]
    phase_tables(info, bases, cosines, sines, angle)

    def pass_on(part, slot, peer):
        return send(every.at[part[0], part[1]], every.at[part[0], part[1]], row_sems, slot, peer)

    up_one.wait_recv()
    far_up = pass_on((lower, one), 5, above)
    side_a = pass_on((lower, one), 6, beside)
    down_two.wait_recv()
    far_down = pass_on((upper, two), 7, below)
    side_b = pass_on((upper, two), 8, beside)
    up_two.wait_recv()
    side_c = pass_on((lower, two), 9, beside)
    down_one.wait_recv()
    side_d = pass_on((upper, one), 10, beside)
    far_up.wait_recv()
    side_e = pass_on((across, one), 11, beside)
    far_down.wait_recv()
    side_f = pass_on((across, two), 12, beside)
    for copy in (side, side_a, side_b, side_c, side_d, side_e, side_f) + tuple(third):
        copy.wait()
    for copy in (up_one, down_two, up_two, down_one, far_up, far_down):
        copy.wait_send()


def gradient_kernel(
    counts, pos_z, pos_x, ext, probe, data, right_f, left_f, left_b, right_b, grad, parts, rims, probe_acc,
):
    count = counts[0, 0]
    grad[...] = jnp.zeros_like(grad)
    probe_acc[...] = jnp.zeros_like(probe_acc)
    lane = lanes((PS, TW))

    def sheet(values, axis):
        return jnp.concatenate(values, axis=axis)

    def group(index, carry):
        probe_real, probe_imag = probe[0], probe[1]
        rows, windows, spots = [], [], []
        for offset in range(GROUP):
            slot = GROUP * index + offset
            start_z, start_x = pos_z[0, 0, slot], pos_x[0, 0, slot]
            back = lax.rem(TW - start_x, TW)
            here = pl.ds(start_z, PS)
            real, imag = (
                pltpu.roll(jnp.where(lane >= start_x, ext[0, part, here, :], ext[1, part, here, :]), back, 1)
                for part in range(2)
            )
            windows.append((real, imag))
            spots.append((slot, start_z, start_x))
            rows.append(sheet(times((probe_real, probe_imag), (real, imag)), 1))
        turned = dot_right(sheet(rows, 0), right_f[...])
        turned = [turned[s * PS : (s + 1) * PS] for s in range(GROUP)]
        far = dot_left(left_f[...], sheet([sheet([v[:, :PS], v[:, PS:]], 0) for v in turned], 1))
        weighted = []
        for s in range(GROUP):
            slot = spots[s][0]
            far_real, far_imag = far[:PS, s * PS : (s + 1) * PS], far[PS:, s * PS : (s + 1) * PS]
            live = jnp.where(slot < count, 1.0, 0.0).astype(F32)
            misfit = (far_real * far_real + far_imag * far_imag - data[slot]) * live
            weighted.append(sheet([misfit * far_real, misfit * far_imag], 0))
        turned = dot_left(left_b[...], sheet(weighted, 1))
        turned = [turned[:, s * PS : (s + 1) * PS] for s in range(GROUP)]
        chi = dot_right(sheet([sheet([v[:PS], v[PS:]], 1) for v in turned], 0), right_b[...])
        for s in range(GROUP):
            slot, start_z, start_x = spots[s]
            here = pl.ds(start_z, PS)
            chi_real, chi_imag = chi[s * PS : (s + 1) * PS, :PS], chi[s * PS : (s + 1) * PS, PS:]
            real, imag = windows[s]
            probe_acc[pl.ds(0, PS), :] += real * chi_real + imag * chi_imag
            probe_acc[pl.ds(PS, PS), :] += real * chi_imag - imag * chi_real
            grad_real = probe_real * chi_real + probe_imag * chi_imag
            grad_imag = probe_real * chi_imag - probe_imag * chi_real
            for part, value in ((0, grad_real), (1, grad_imag)):
                moved = pltpu.roll(value, start_x, 1)
                grad[0, part, here, :] += jnp.where(lane >= start_x, moved, 0.0)
                grad[1, part, here, :] += jnp.where(lane < start_x, moved, 0.0)
        return carry

    lax.fori_loop(0, (count + GROUP - 1) // GROUP, group, 0)
    for chunk in range(ANG):
        parts[chunk] = probe_acc[pl.ds(chunk * CHUNK, CHUNK), :]
    low = lanes((ROWS, TW)) < HALF
    rims[0] = jnp.where(low, grad[0, 0], pltpu.roll(grad[0, 1], HALF, 1))
    rims[1] = jnp.where(low, pltpu.roll(grad[1, 0], HALF, 1), grad[1, 1])


def phase_tables(info, bases, cosines, sines, here):
    frequency = sublanes((TILES, TW)) + TILES * lanes((TILES, TW))
    signed = jnp.where(frequency < H // 2, frequency, frequency - H).astype(F32)
    centre = (YB * here - ANG * YB // 2).astype(F32) + (YB - 1) / 2.0
    row = sublanes((8, TW))
    for angle in range(ANG):
        turn = signed * (1.0 / H) * info[pl.ds(1, 1), pl.ds(angle, 1)]
        whole = centre * turn
        whole = 2.0 * math.pi * (whole - jnp.round(whole))
        half = math.pi * turn
        bases[angle, 0], bases[angle, 1] = jnp.cos(whole), jnp.sin(whole)
        power = (jnp.cos(half), jnp.sin(half))
        for level in range(5):
            bases[angle, 2 + 2 * level], bases[angle, 3 + 2 * level] = power
            power = times(power, power)

    def fill(angle, carry):
        for order in range(TILES):
            line = [
                tuple(
                    jnp.broadcast_to(bases[angle, 2 + 2 * level + part, pl.ds(order, 1), :], (8, TW))
                    for part in range(2)
                )
                for level in range(5)
            ]
            now = line[0]
            for level in range(3):
                ahead = times(now, line[1 + level])
                chosen = (row & (1 << level)) != 0
                now = tuple(jnp.where(chosen, new, old) for new, old in zip(ahead, now))
            later = times(now, line[4])
            cosines[angle, order, pl.ds(0, 8), :], sines[angle, order, pl.ds(0, 8), :] = now
            cosines[angle, order, pl.ds(8, 8), :], sines[angle, order, pl.ds(8, 8), :] = later
        return carry

    lax.fori_loop(0, ANG, fill, 0)


def flip8(value):
    row = sublanes(value.shape)
    value = pltpu.roll(value, 4, 0)
    value = jnp.where((row & 2) == 0, pltpu.roll(value, 6, 0), pltpu.roll(value, 2, 0))
    return jnp.where((row & 1) == 0, pltpu.roll(value, 7, 0), pltpu.roll(value, 1, 0))


def image_kernel(
    rows, bases, cosines, sines, turns, right_b, probe0, gathered, info, psi,
    image, probe_new, psi_new, turned, spread, middle, ready, sems,
):
    number = info[pl.ds(0, 1), pl.ds(0, 1)]
    for chunk in range(ANG):
        part, start = divmod(chunk * CHUNK, PS)
        here = pl.ds(start, CHUNK)
        probe_new[part, here, :] = probe0[part, here, :] - PROBE_STEP * gathered[chunk] / number
    psi_new[...] = psi[...]

    def shear(z):
        for angle in range(ANG):
            value = (rows[angle, z, :, pl.ds(0, TW)], rows[angle, z, :, pl.ds(TW, TW)])
            turned[angle, 0], turned[angle, 1] = times(value, (bases[angle, 0], bases[angle, 1]))
        for order in range(TILES):
            sums = None
            for angle in range(ANG):
                real = jnp.broadcast_to(turned[angle, 0, pl.ds(order, 1), :], (16, TW))
                imag = jnp.broadcast_to(turned[angle, 1, pl.ds(order, 1), :], (16, TW))
                cosine, sine = cosines[angle, order], sines[angle, order]
                terms = (real * cosine, imag * sine, real * sine, imag * cosine)
                sums = terms if sums is None else tuple(s + t for s, t in zip(sums, terms))
            rc, isn, rs, ic = sums
            above = (rc - isn, rs + ic)
            below = (rc + isn, ic - rs)
            for part in range(2):
                back = jnp.concatenate([flip8(below[part][8:]), flip8(below[part][:8])], axis=0)
                value = jnp.concatenate([back, above[part]], axis=0)
                high, low = split(value)
                here = pl.ds(order * YB, YB)
                spread[here, pl.ds(part * TW, TW)] = high
                spread[here, pl.ds((2 + part) * TW, TW)] = low
                spread[here, pl.ds((4 + part) * TW, TW)] = high

    def finish(slot):
        middle[...] = jnp.dot(spread[...], right_b[...], preferred_element_type=F32)
        for group in range(YB // 16):
            items = []
            for order in range(TILES):
                here = pl.ds(order * YB + 16 * group, 16)
                value = (middle[here, pl.ds(0, TW)], middle[here, pl.ds(TW, TW)])
                turn = (turns[0, pl.ds(order, 1), :], turns[1, pl.ds(order, 1), :])
                items.append(times(value, turn))
            for tile, item in enumerate(sixteen(items, 1)):
                for part in range(2):
                    ready[slot, part, pl.ds(16 * group, 16), pl.ds(tile * TW, TW)] = item[part].astype(BF16)

    def put(slot, z):
        return [
            pltpu.make_async_copy(ready.at[slot, part], image.at[part, z], sems.at[slot, part]) for part in range(2)
        ]

    def step(pair, carry):
        for slot in range(2):
            z = 2 * pair + slot
            shear(z)

            @pl.when(pair > 0)
            def _():
                for copy in put(slot, z - 2):
                    copy.wait()

            finish(slot)
            for copy in put(slot, z):
                copy.start()
        return carry

    lax.fori_loop(0, ZS // 2, step, 0)
    for slot in range(2):
        for copy in put(slot, ZS - 2 + slot):
            copy.wait()


def arr(*shape):
    return jax.ShapeDtypeStruct(shape, F32)


def dma(*shape):
    return pltpu.SemaphoreType.DMA(shape)


def call(kernel, outs, specs, out_specs, scratch, ident=None):
    extra = {} if ident is None else {"collective_id": ident, "has_side_effects": True}
    return pl.pallas_call(
        kernel,
        out_shape=outs,
        in_specs=specs,
        out_specs=out_specs,
        scratch_shapes=scratch,
        compiler_params=pltpu.CompilerParams(vmem_limit_bytes=VLIMIT, **extra),
    )


def shards(psi, target, probe, data, pos_z, pos_x, counts, shears):
    psi, target = psi.reshape(2, ROWS, TW), target.reshape(2, ROWS, TW)
    data = data.reshape(CAP, PS, PS)
    unit = dft_block(PS, 1.0 / math.sqrt(PS))
    tables = [
        jnp.asarray(t)
        for t in (right_table(unit), left_table(unit.T), left_table(unit), right_table(unit.T))
    ]
    wide, edge, small = arr(2, 2, ROWS, TW), arr(2, ROWS, TW), arr(8, TW)
    chunks, square = arr(ANG, CHUNK, TW), arr(2, PS, PS)
    table_shapes = [jax.ShapeDtypeStruct(t.shape, t.dtype) for t in tables]
    one = lambda *shape: pltpu.VMEM(shape, F32)

    outs = [wide, edge, edge, small, square, arr(CAP, PS, PS)] + table_shapes
    ext, goal, packs, info, probe, data, *tables = call(
        halo_kernel,
        outs,
        [SMEM] * 2 + [HBM] * 8,
        [VMEM] * len(outs),
        [
            one(2, ROWS, TW), one(2, ROWS, TW), one(ROWS, TW), one(ROWS, TW), one(8, TW), one(ANG, 8, TW),
            dma(2, 2), dma(2, ANG), dma(8),
        ],
        0,
    )(counts, shears, *(pltpu.with_memory_space_constraint(x, pltpu.HBM) for x in (psi, target, probe, data, *tables)))

    def gradient(ext, probe):
        return call(
            gradient_kernel, [wide, chunks, edge], [SMEM] * 3 + [VMEM] * 7, [VMEM] * 3, [one(2 * PS, PS)]
        )(counts, pos_z, pos_x, ext, probe, data, *tables)

    grad, parts, rims = gradient(ext, probe)
    ext, probe, info_all = call(
        exchange_kernel,
        [wide, square, small],
        [VMEM] * 7,
        [VMEM] * 3,
        [
            one(2, ROWS, TW), one(2, ROWS, TW), one(ROWS, TW), one(ROWS, TW),
            one(ANG, CHUNK, TW), one(CHUNK, TW), one(TILES, CHUNK, TW), one(CHUNK, TW), one(ANG, CHUNK, TW), one(TILES, 8, TW),
            dma(2, 2), dma(2, 2), dma(2, ANG), dma(2, TILES), dma(2, ANG), dma(2, TILES),
        ],
        1,
    )(grad, parts, packs, info, ext, goal, probe)
    grad, parts, rims = gradient(ext, probe)
    every, phases = arr(ANG, ZS, TILES, WIDE), arr(ANG, TILES, 16, TW)
    psi_new, every, gathered, bases, cosines, sines = call(
        tail_kernel,
        [edge, every, chunks, arr(ANG, 12, TILES, TW), phases, phases],
        [VMEM] * 8,
        [VMEM] * 6,
        [
            one(ROWS, TW), one(ROWS, TW),
            one(ANG, CHUNK, TW), one(CHUNK, TW), one(TILES, CHUNK, TW), one(CHUNK, TW),
            one(TILES, 2, ZS, TW), one(TILES, 2, ZS, TW), one(WIDE, WIDE), one(ZS, TILES, WIDE),
            dma(2, 2), dma(2, ANG), dma(2, TILES), dma(2, ANG), dma(2, TILES), dma(2, 13),
        ],
        2,
    )(ext, goal, grad, rims, parts, info, jnp.asarray(turn_table(-1)), jnp.asarray(right_table(dft_block(TW, 1.0))))
    inverse = dft_block(TW, 1.0 / (H * ANG)).T
    image, probe_new, psi_new = call(
        image_kernel,
        [jax.ShapeDtypeStruct((2, ZS, YB, H), BF16), square, edge],
        [VMEM] * 10,
        [HBM, VMEM, VMEM],
        [
            one(ANG, 2, TILES, TW),
            pltpu.VMEM((TILES * YB, 3 * WIDE), BF16),
            one(TILES * YB, WIDE),
            pltpu.VMEM((2, 2, YB, H), BF16),
            dma(2, 2),
        ],
    )(
        every, bases, cosines, sines, jnp.asarray(turn_table(1)), jnp.asarray(right_table(inverse)),
        probe, gathered, info_all, psi_new,
    )
    return psi_new.reshape(2, 1, ROWS, TW), probe_new, image


def solution(mesh):
    in_specs = (
        P(None, "angle", None, "tile"),
        P(None, "angle", None, "tile"),
        P(),
        P("angle", "tile", None, None, None),
        P("angle", "tile", None),
        P("angle", "tile", None),
        P("angle", "tile"),
        P("angle"),
    )
    out_specs = (P(None, "angle", None, "tile"), P(), P(None, "tile", "angle", None))
    return jax.shard_map(shards, mesh=mesh, in_specs=in_specs, out_specs=out_specs, check_vma=False)
```

time: 123 us -> 86.6 us (0.70)
  Pallas kernels: 121 us -> 84.1 us
    pallas_call x10 -> x6, Pallas kernels: 121 us -> 84.1 us  [the longest x1 28.6 us: shards(): call(tail_kernel, [edge, every, chunks, arr(ANG, 12, TILES, TW), phases,...]
where the time goes in v2:
time: 86.6 us; the launch traced here: 86.2 us
  Pallas kernels  84.1 us (97%)
  between operations  2.05 us (2%)
    pallas_call x1, Pallas kernels, shards(): call(tail_kernel, [edge, every, chunks, arr(ANG, 12, TILES, TW), phases,...  28.6 us
    pallas_call x1, Pallas kernels, shards(): call(exchange_kernel, [wide, square, small], [VMEM] * 7, [VMEM] * 3, [one...  23.8 us
    pallas_call x1, Pallas kernels, shards(): call(halo_kernel, outs, [SMEM] * 2 + [HBM] * 8, [VMEM] * len(outs), [one(...  14.2 us
    pallas_call x1, Pallas kernels, shards(): call(image_kernel, [jax.ShapeDtypeStruct((2, ZS, YB, H), BF16), square, e...  11.7 us
    pallas_call x2, Pallas kernels, gradient(): call(gradient_kernel, [wide, chunks, edge], [SMEM] * 3 + [VMEM] * 7, [VME...  5.76 us

profile of v2, /device:TPU:1, one launch (start us, length us, event | category | flops | bytes accessed | tf_op | source)
XLA Modules:
  0.0 86.2 jit_solution(13683999390761202439)
XLA Ops:
  0.6 0.0 copy-start.5
  0.6 0.0 copy-start.4
  2.0 14.2 %shard_map.175 = (f32[2,2,160,128]{3,2,1,0:T(8,128)S(1)}, f32[2,160,128]{2,1,0:T(8,128)S(1)}, f32[2,160,128]{2,1,0:T(8,128)S(1)}, f32[8,128]{1,0:T(8,128)S(1)}, ...) custom-call(s32[1,1]{1,0:T(1,128)S(6)} %copy.20.counts, ...), custom_call_target="tpu_custom_call" | custom-call | tf_op jit(solution)/shard_map/pallas_call | solution.py:619
  16.2 0.0 copy-done.5
  16.2 0.0 copy-done.4
  16.2 3.2 %shard_map.176 = (f32[2,2,160,128]{3,2,1,0:T(8,128)S(1)}, f32[8,32,128]{2,1,0:T(8,128)S(1)}, f32[2,160,128]{2,1,0:T(8,128)}) custom-call(s32[1,1]{1,0:T(1,128)S(6)} %copy.20.counts, s32[1,1,16]{2,1,0:T(1,128)S(1)} %copy-done.4, s32[1,1,16]{2,1,0:T(1,128)S(1)} %copy-done.5, f32[2,2,160,128]{3,2,1,0:T(8,128)S(1)} %get-tuple-element.30.ext.ext0, ...), custom_call_target="tpu_custom_call" | custom-call | tf_op jit(solution)/shard_map/pallas_call | solution.py:632
  19.4 0.0 copy-start.1
  19.4 0.0 copy-start.3
  19.4 23.8 %shard_map.177 = (f32[2,2,160,128]{3,2,1,0:T(8,128)S(1)}, f32[2,128,128]{2,1,0:T(8,128)S(1)}, f32[8,128]{1,0:T(8,128)S(1)}) custom-call(f32[2,2,160,128]{3,2,1,0:T(8,128)S(1)} %get-tuple-element.37.grad, f32[8,32,128]{2,1,0:T(8,128)S(1)} %get-tuple-element.38.parts, f32[2,160,128]{2,1,0:T(8,128)S(1)} %get-tuple-element.39.packs, ...), custom_call_target="tpu_custom_call" | custom-call | tf_op jit(solution)/shard_map/pallas_call | solution.py:637
  43.3 0.0 copy-start
  43.3 0.0 copy-start.2
  43.3 2.5 %shard_map.178 = (f32[2,2,160,128]{3,2,1,0:T(8,128)S(1)}, f32[8,32,128]{2,1,0:T(8,128)S(1)}, f32[2,160,128]{2,1,0:T(8,128)S(1)}) custom-call(s32[1,1]{1,0:T(1,128)S(6)} %copy.20.counts, s32[1,1,16]{2,1,0:T(1,128)S(1)} %copy-done.4, s32[1,1,16]{2,1,0:T(1,128)S(1)} %copy-done.5, f32[2,2,160,128]{3,2,1,0:T(8,128)S(1)} %get-tuple-element.42.ext, ...), custom_call_target="tpu_custom_call" | custom-call | tf_op jit(solution)/shard_map/pallas_call | solution.py:632
  45.8 0.0 copy-done.1
  45.8 0.0 copy-done.3
  45.8 28.6 %shard_map.179 = (f32[2,160,128]{2,1,0:T(8,128)S(1)}, f32[8,10,16,256]{3,2,1,0:T(8,128)S(1)}, f32[8,32,128]{2,1,0:T(8,128)S(1)}, f32[8,12,16,128]{3,2,1,0:T(8,12...) custom-call(f32[2,2,160,128]{3,2,1,0:T(8,128)S(1)} %get-tuple-element.42.ext, ...), custom_call_target="tpu_custom_call" | custom-call | tf_op jit(solution)/shard_map/pallas_call | solution.py:651
  74.4 0.0 copy-done
  74.5 0.0 copy-done.2
  74.5 11.7 %shard_map.180 = (bf16[2,10,32,2048]{3,2,1,0:T(8,128)(2,1)}, f32[2,128,128]{2,1,0:T(8,128)}, f32[2,160,128]{2,1,0:T(8,128)}) custom-call(f32[8,10,16,256]{3,2,1,0:T(8,128)S(1)} %get-tuple-element.47.rows, f32[8,12,16,128]{3,2,1,0:T(8,128)S(1)} %get-tuple-element.48.bases, f32[8,16,16,128]{3,2,1,0:T(8,128)S(1)} %get-tuple-element.49.cosines, ...), custom_call_target="tpu_custom_call" | custom-call | tf_op jit(solution)/shard_map/pallas_call | solution.py:665
Async XLA Ops:
  0.6 15.6 %copy-start.5 = (s32[1,1,16]{2,1,0:T(1,128)S(1)}, s32[1,1,16]{2,1,0:T(1,128)}, u32[]{:S(2)}) copy-start(s32[1,1,16]{2,1,0:T(1,128)} %pos_x.3) | copy-start | bytes 196
  0.6 15.6 %copy-start.4 = (s32[1,1,16]{2,1,0:T(1,128)S(1)}, s32[1,1,16]{2,1,0:T(1,128)}, u32[]{:S(2)}) copy-start(s32[1,1,16]{2,1,0:T(1,128)} %pos_z.3) | copy-start | bytes 196
  19.4 26.4 %copy-start.1 = (bf16[768,256]{1,0:T(8,128)(2,1)S(1)}, bf16[768,256]{1,0:T(8,128)(2,1)}, u32[]{:S(2)}) copy-start(bf16[768,256]{1,0:T(8,128)(2,1)} %constant.21.clone.right_f) | copy-start | bytes 1179652
  19.4 26.4 %copy-start.3 = (f32[2,16,128]{2,1,0:T(8,128)S(1)}, f32[2,16,128]{2,1,0:T(8,128)}, u32[]{:S(2)}) copy-start(f32[2,16,128]{2,1,0:T(8,128)} %constant.20.clone.turns) | copy-start | bytes 49156
  43.3 31.2 %copy-start = (bf16[768,256]{1,0:T(8,128)(2,1)S(1)}, bf16[768,256]{1,0:T(8,128)(2,1)}, u32[]{:S(2)}) copy-start(bf16[768,256]{1,0:T(8,128)(2,1)} %constant.23.clone.right_b) | copy-start | bytes 1179652
  43.3 31.2 %copy-start.2 = (f32[2,16,128]{2,1,0:T(8,128)S(1)}, f32[2,16,128]{2,1,0:T(8,128)}, u32[]{:S(2)}) copy-start(f32[2,16,128]{2,1,0:T(8,128)} %constant.22.clone.turns) | copy-start | bytes 49156

commit v3 on v2

--- a/solution.py
+++ b/solution.py
@@ -26,7 +26,7 @@
 YB = 32
 H = 2048
 CHUNK = 2 * PS // ANG
-GROUP = 4
+GROUP = 8
 
 F32 = jnp.float32
 BF16 = jnp.bfloat16
@@ -97,6 +97,22 @@
     return [first, plus, third, minus] if orient > 0 else [first, minus, third, plus]
 
 
+def turn_by(value, step, orient):
+    real, imag = value
+    if orient < 0:
+        real, imag = imag, real
+    if step == 4:
+        real, imag = -imag, real
+    elif step == 2:
+        real, imag = (real - imag) * math.sqrt(0.5), (real + imag) * math.sqrt(0.5)
+    elif step == 6:
+        real, imag = (real + imag) * -math.sqrt(0.5), (real - imag) * math.sqrt(0.5)
+    else:
+        angle = 2.0 * math.pi * step / 16
+        real, imag = times((real, imag), (math.cos(angle), math.sin(angle)))
+    return (imag, real) if orient < 0 else (real, imag)
+
+
 def sixteen(items, orient):
     columns = []
     for fine in range(4):
@@ -104,8 +120,7 @@
         for order in range(1, 4):
             step = fine * order
             if step:
-                angle = orient * 2.0 * math.pi * step / 16
-                partial[order] = times(partial[order], (math.cos(angle), math.sin(angle)))
+                partial[order] = turn_by(partial[order], step, orient)
         columns.append(partial)
     result = [None] * 16
     for low in range(4):
@@ -160,11 +175,52 @@
 
 
 def start_edges(packs, from_left, from_right, sems, angle, tile):
+    def copy(side, landing, peer):
+        return pltpu.make_async_remote_copy(
+            src_ref=packs.at[side],
+            dst_ref=landing,
+            send_sem=sems.at[0, side],
+            recv_sem=sems.at[1, side],
+            device_id=peer,
+            device_id_type=MESH,
+        )
+
     left, right = neighbours(angle, tile)
-    return [
-        send(packs.at[0], from_right, sems, 0, left),
-        send(packs.at[1], from_left, sems, 1, right),
-    ]
+    to_left, to_right = copy(0, from_right, left), copy(1, from_left, right)
+
+    @pl.when(tile > 0)
+    def _():
+        to_left.start()
+
+    @pl.when(tile < TILES - 1)
+    def _():
+        to_right.start()
+
+    return to_left, to_right
+
+
+def finish_edges(copies, tile):
+    to_left, to_right = copies
+
+    @pl.when(tile > 0)
+    def _():
+        to_left.wait_send()
+        to_right.wait_recv()
+
+    @pl.when(tile < TILES - 1)
+    def _():
+        to_right.wait_send()
+        to_left.wait_recv()
+
+
+def clear_edges(from_left, from_right, tile):
+    @pl.when(tile == 0)
+    def _():
+        from_left[...] = jnp.zeros_like(from_left)
+
+    @pl.when(tile == TILES - 1)
+    def _():
+        from_right[...] = jnp.zeros_like(from_right)
 
 
 def start_first(parts, landed, sems, angle, tile):
@@ -215,10 +271,8 @@
     )
 
 
-def widened(real, imag, before, after, tile):
+def widened(real, imag, before, after):
     low = lanes((ROWS, TW)) < HALF
-    before = jnp.where(tile > 0, before, 0.0)
-    after = jnp.where(tile < TILES - 1, after, 0.0)
     real, imag = pltpu.roll(real, HALF, 1), pltpu.roll(imag, HALF, 1)
     return (
         (jnp.where(low, before, real), jnp.where(low, pltpu.roll(before, HALF, 1), imag)),
@@ -248,6 +302,7 @@
     fetches[0].wait()
     for side, value in enumerate(packed_sides(own[0], own[1])):
         sides[side] = value
+    clear_edges(from_left, from_right, tile)
     meet(angle_peers(angle, tile) + list(neighbours(angle, tile)))
     edges = start_edges(sides, from_left, from_right, edge_sems, angle, tile)
     infos = [
@@ -258,9 +313,8 @@
         packs[side] = value
     for fetch in fetches[2:]:
         fetch.wait()
-    for copy in edges:
-        copy.wait()
-    for side, pair in enumerate(widened(own[0], own[1], from_left[...], from_right[...], tile)):
+    finish_edges(edges, tile)
+    for side, pair in enumerate(widened(own[0], own[1], from_left[...], from_right[...])):
         for part in range(2):
             ext[side, part] = pair[part]
     for copy in infos:
@@ -277,6 +331,8 @@
     edge_sems, goal_sems, first_sems, second_sems, third_sems, info_sems,
 ):
     angle, tile = place()
+    clear_edges(from_left, from_right, tile)
+    clear_edges(goal_left, goal_right, tile)
     meet(angle_peers(angle, tile) + tile_peers(angle, tile))
     first = start_first(parts, landed_first, first_sems, angle, tile)
     edges = start_edges(grad, from_left, from_right, edge_sems, angle, tile)
@@ -284,14 +340,14 @@
     goals = start_edges(packs, goal_left, goal_right, goal_sems, angle, tile)
     first_sum[...] = finish_first(first, parts, landed_first, angle)
     second = start_second(first_sum, landed_second, second_sems, angle, tile)
-    for copy in edges + goals:
-        copy.wait()
+    finish_edges(edges, tile)
+    finish_edges(goals, tile)
     low = lanes((ROWS, TW)) < HALF
     inner, outer = tile > 0, tile < TILES - 1
-    goal = widened(own_target[0], own_target[1], goal_left[...], goal_right[...], tile)
+    goal = widened(own_target[0], own_target[1], goal_left[...], goal_right[...])
     for side, landed, inside in ((0, from_left, inner), (1, from_right, outer)):
         for part in range(2):
-            total = grad[side, part] + jnp.where(inside, landed[part], 0.0)
+            total = grad[side, part] + landed[part]
             old = ext0[side, part]
             new = old - ALPHA * (total + RHO * (old - goal[side][part]))
             keep = jnp.logical_or(inside, jnp.logical_not(low) if side == 0 else low)
@@ -316,43 +372,46 @@
     edge_sems, first_sems, second_sems, third_sems, slab_sems, row_sems,
 ):
     angle, tile = place()
-    meet(angle_peers(angle, tile) + tile_peers(angle, tile))
-    edges = start_edges(rims, from_left, from_right, edge_sems, angle, tile)
-    first = start_first(parts, landed_first, first_sems, angle, tile)
+    clear_edges(from_left, from_right, tile)
     low = lanes((ROWS, TW)) < HALF
-    inner, outer = tile > 0, tile < TILES - 1
     for part in range(2):
         old, total = (
             jnp.where(low, pltpu.roll(wide[0, part], HALF, 1), pltpu.roll(wide[1, part], HALF, 1))
             for wide in (ext, grad)
         )
-        psi_new[part] = old - ALPHA * (total + RHO * (old - own_target[part]))
-    for copy in edges:
-        copy.wait()
-    for part in range(2):
-        before = jnp.where(inner, from_left[...], 0.0)
-        after = jnp.where(outer, from_right[...], 0.0)
-        if part == 0:
-            extra = jnp.where(low, before, pltpu.roll(after, HALF, 1))
-        else:
-            extra = jnp.where(low, pltpu.roll(before, HALF, 1), after)
-        new = psi_new[part] - ALPHA * extra
+        new = old - ALPHA * (total + RHO * (old - own_target[part]))
         psi_new[part] = new
-        gap = own_target[part] - new
-        for slab in range(TILES):
-            slabs[slab, part] = gap[slab * ZS : (slab + 1) * ZS]
+        for source, first_row in ((own_target[part] - new, part * ZS), (rims[part], (2 + part) * ZS)):
+            for slab in range(TILES):
+                slabs[slab, pl.ds(first_row, ZS), :] = source[slab * ZS : (slab + 1) * ZS]
+    meet(angle_peers(angle, tile) + tile_peers(angle, tile))
     copies = []
     for step in range(1, TILES):
         owner = (tile + step) % TILES
         copies.append(send(slabs.at[owner], slabs_here.at[tile], slab_sems, step, (angle, owner)))
+    first = start_first(parts, landed_first, first_sems, angle, tile)
+    edges = start_edges(rims, from_left, from_right, edge_sems, angle, tile)
     slabs_here[tile] = slabs[tile]
+    work[...] = jnp.zeros_like(work)
     first_sum[...] = finish_first(first, parts, landed_first, angle)
     second = start_second(first_sum, landed_second, second_sems, angle, tile)
     for copy in copies:
         copy.wait()
 
-    items = [(slabs_here[index, 0], slabs_here[index, 1]) for index in range(TILES)]
-    work[...] = jnp.zeros_like(work)
+    low = lanes((ZS, TW)) < HALF
+    zero = jnp.zeros((ZS, TW), F32)
+    items = []
+    for index in range(TILES):
+        before = slabs_here[index - 1, pl.ds(3 * ZS, ZS), :] if index else zero
+        after = slabs_here[index + 1, pl.ds(2 * ZS, ZS), :] if index < TILES - 1 else zero
+        real = jnp.where(low, before, pltpu.roll(after, HALF, 1))
+        imag = jnp.where(low, pltpu.roll(before, HALF, 1), after)
+        items.append(
+            (
+                slabs_here[index, pl.ds(0, ZS), :] + ALPHA * real,
+                slabs_here[index, pl.ds(ZS, ZS), :] + ALPHA * imag,
+            )
+        )
     for order, item in enumerate(sixteen(items, -1)):
         turn = (turns[0, pl.ds(order, 1), :], turns[1, pl.ds(order, 1), :])
         real, imag = times(item, turn)
@@ -376,6 +435,15 @@
     second_sum[...] = finish_second(second, first_sum, landed_second, tile)
     third = start_third(second_sum, gathered, third_sems, angle, tile)
     gathered[angle] = second_sum[...]
+    finish_edges(edges, tile)
+    for part in range(2):
+        before, after = from_left[...], from_right[...]
+        low = lanes((ROWS, TW)) < HALF
+        if part == 0:
+            extra = jnp.where(low, before, pltpu.roll(after, HALF, 1))
+        else:
+            extra = jnp.where(low, pltpu.roll(before, HALF, 1), after)
+        psi_new[part] = psi_new[part] - ALPHA * extra
     phase_tables(info, bases, cosines, sines, angle)
 
     def pass_on(part, slot, peer):
@@ -427,23 +495,25 @@
             windows.append((real, imag))
             spots.append((slot, start_z, start_x))
             rows.append(sheet(times((probe_real, probe_imag), (real, imag)), 1))
-        turned = dot_right(sheet(rows, 0), right_f[...])
-        turned = [turned[s * PS : (s + 1) * PS] for s in range(GROUP)]
-        far = dot_left(left_f[...], sheet([sheet([v[:, :PS], v[:, PS:]], 0) for v in turned], 1))
+        pairs = range(0, GROUP, 2)
+        sides = (slice(0, PS), slice(PS, 2 * PS))
+        turned = [dot_right(sheet(rows[p : p + 2], 0), right_f[...]) for p in pairs]
+        turned = [sheet([sheet([v[k, :PS], v[k, PS:]], 0) for k in sides], 1) for v in turned]
+        far = [dot_left(left_f[...], v) for v in turned]
         weighted = []
         for s in range(GROUP):
             slot = spots[s][0]
-            far_real, far_imag = far[:PS, s * PS : (s + 1) * PS], far[PS:, s * PS : (s + 1) * PS]
+            far_real, far_imag = (far[s // 2][k, sides[s % 2]] for k in sides)
             live = jnp.where(slot < count, 1.0, 0.0).astype(F32)
             misfit = (far_real * far_real + far_imag * far_imag - data[slot]) * live
             weighted.append(sheet([misfit * far_real, misfit * far_imag], 0))
-        turned = dot_left(left_b[...], sheet(weighted, 1))
-        turned = [turned[:, s * PS : (s + 1) * PS] for s in range(GROUP)]
-        chi = dot_right(sheet([sheet([v[:PS], v[PS:]], 1) for v in turned], 0), right_b[...])
+        turned = [dot_left(left_b[...], sheet(weighted[p : p + 2], 1)) for p in pairs]
+        turned = [sheet([sheet([v[:PS, k], v[PS:, k]], 1) for k in sides], 0) for v in turned]
+        chi = [dot_right(v, right_b[...]) for v in turned]
         for s in range(GROUP):
             slot, start_z, start_x = spots[s]
             here = pl.ds(start_z, PS)
-            chi_real, chi_imag = chi[s * PS : (s + 1) * PS, :PS], chi[s * PS : (s + 1) * PS, PS:]
+            chi_real, chi_imag = (chi[s // 2][sides[s % 2], k] for k in sides)
             real, imag = windows[s]
             probe_acc[pl.ds(0, PS), :] += real * chi_real + imag * chi_imag
             probe_acc[pl.ds(PS, PS), :] += real * chi_imag - imag * chi_real
@@ -510,7 +580,7 @@
 
 def image_kernel(
     rows, bases, cosines, sines, turns, right_b, probe0, gathered, info, psi,
-    image, probe_new, psi_new, turned, spread, middle, ready, sems,
+    image, probe_new, psi_new, turned_a, turned_b, spread_a, spread_b, middle_a, middle_b, ready, sems,
 ):
     number = info[pl.ds(0, 1), pl.ds(0, 1)]
     for chunk in range(ANG):
@@ -519,7 +589,7 @@
         probe_new[part, here, :] = probe0[part, here, :] - PROBE_STEP * gathered[chunk] / number
     psi_new[...] = psi[...]
 
-    def shear(z):
+    def shear(z, turned, spread):
         for angle in range(ANG):
             value = (rows[angle, z, :, pl.ds(0, TW)], rows[angle, z, :, pl.ds(TW, TW)])
             turned[angle, 0], turned[angle, 1] = times(value, (bases[angle, 0], bases[angle, 1]))
@@ -543,7 +613,7 @@
                 spread[here, pl.ds((2 + part) * TW, TW)] = low
                 spread[here, pl.ds((4 + part) * TW, TW)] = high
 
-    def finish(slot):
+    def finish(slot, spread, middle):
         middle[...] = jnp.dot(spread[...], right_b[...], preferred_element_type=F32)
         for group in range(YB // 16):
             items = []
@@ -562,23 +632,37 @@
         ]
 
     def step(pair, carry):
-        for slot in range(2):
-            z = 2 * pair + slot
-            shear(z)
-
-            @pl.when(pair > 0)
-            def _():
-                for copy in put(slot, z - 2):
+        base = 2 * lax.rem(pair, 2)
+
+        @pl.when(pair > 1)
+        def _():
+            for odd in range(2):
+                for copy in put(base + odd, 2 * pair - 4 + odd):
                     copy.wait()
 
-            finish(slot)
-            for copy in put(slot, z):
+        shear(2 * pair + 1, turned_b, spread_b)
+        finish(base, spread_a, middle_a)
+        shear(2 * pair + 2, turned_a, spread_a)
+        finish(base + 1, spread_b, middle_b)
+        for odd in range(2):
+            for copy in put(base + odd, 2 * pair + odd):
                 copy.start()
         return carry
 
-    lax.fori_loop(0, ZS // 2, step, 0)
-    for slot in range(2):
-        for copy in put(slot, ZS - 2 + slot):
+    shear(0, turned_a, spread_a)
+    lax.fori_loop(0, ZS // 2 - 1, step, 0)
+    for odd in range(2):
+        for copy in put(odd, ZS - 6 + odd):
+            copy.wait()
+    shear(ZS - 1, turned_b, spread_b)
+    finish(0, spread_a, middle_a)
+    for copy in put(0, ZS - 2):
+        copy.start()
+    finish(1, spread_b, middle_b)
+    for copy in put(1, ZS - 1):
+        copy.start()
+    for slot, z in ((2, ZS - 4), (3, ZS - 3), (0, ZS - 2), (1, ZS - 1)):
+        for copy in put(slot, z):
             copy.wait()
 
 
@@ -656,7 +740,7 @@
         [
             one(ROWS, TW), one(ROWS, TW),
             one(ANG, CHUNK, TW), one(CHUNK, TW), one(TILES, CHUNK, TW), one(CHUNK, TW),
-            one(TILES, 2, ZS, TW), one(TILES, 2, ZS, TW), one(WIDE, WIDE), one(ZS, TILES, WIDE),
+            one(TILES, 4 * ZS, TW), one(TILES, 4 * ZS, TW), one(WIDE, WIDE), one(ZS, TILES, WIDE),
             dma(2, 2), dma(2, ANG), dma(2, TILES), dma(2, ANG), dma(2, TILES), dma(2, 13),
         ],
         2,
@@ -669,10 +753,13 @@
         [HBM, VMEM, VMEM],
         [
             one(ANG, 2, TILES, TW),
+            one(ANG, 2, TILES, TW),
+            pltpu.VMEM((TILES * YB, 3 * WIDE), BF16),
             pltpu.VMEM((TILES * YB, 3 * WIDE), BF16),
             one(TILES * YB, WIDE),
-            pltpu.VMEM((2, 2, YB, H), BF16),
-            dma(2, 2),
+            one(TILES * YB, WIDE),
+            pltpu.VMEM((4, 2, YB, H), BF16),
+            dma(4, 2),
         ],
     )(
         every, bases, cosines, sines, jnp.asarray(turn_table(1)), jnp.asarray(right_table(inverse)),

time: 86.6 us -> 78.4 us (0.905); the launches traced: 86.2 us -> 78.9 us
  Pallas kernels: 84.1 us -> 76.8 us
    pallas_call x2, Pallas kernels: 5.76 us -> 12.2 us  [gradient(): call(gradient_kernel, [wide, chunks, edge], [SMEM] * 3 + [VMEM] * 7, [VME...]
    pallas_call x1, Pallas kernels: 28.6 us -> 22.7 us  [shards(): call(tail_kernel, [edge, every, chunks, arr(ANG, 12, TILES, TW), phases,...]
    pallas_call x1, Pallas kernels: 23.8 us -> 19 us  [shards(): call(exchange_kernel, [wide, square, small], [VMEM] * 7, [VMEM] * 3, [one...]
    pallas_call x1, Pallas kernels: 11.7 us -> 9.17 us  [shards(): call(image_kernel, [jax.ShapeDtypeStruct((2, ZS, YB, H), BF16), square, e...]
where the time goes in v3:
time: 78.4 us; the launch traced here: 78.9 us
  Pallas kernels  76.8 us (98%)
  between operations  2.05 us (3%)
    pallas_call x1, Pallas kernels, shards(): call(tail_kernel, [edge, every, chunks, arr(ANG, 12, TILES, TW), phases,...  22.7 us
    pallas_call x1, Pallas kernels, shards(): call(exchange_kernel, [wide, square, small], [VMEM] * 7, [VMEM] * 3, [one...  19 us
    pallas_call x1, Pallas kernels, shards(): call(halo_kernel, outs, [SMEM] * 2 + [HBM] * 8, [VMEM] * len(outs), [one(...  13.6 us
    pallas_call x2, Pallas kernels, gradient(): call(gradient_kernel, [wide, chunks, edge], [SMEM] * 3 + [VMEM] * 7, [VME...  12.2 us
    pallas_call x1, Pallas kernels, shards(): call(image_kernel, [jax.ShapeDtypeStruct((2, ZS, YB, H), BF16), square, e...  9.17 us

profile of v3, /device:TPU:1, one launch (start us, length us, event | category | flops | bytes accessed | tf_op | source)
XLA Modules:
  0.0 78.9 jit_solution(7497833516551108010)
XLA Ops:
  0.6 0.0 copy-start.5
  0.6 0.0 copy-start.4
  2.0 13.6 %shard_map.175 = (f32[2,2,160,128]{3,2,1,0:T(8,128)S(1)}, f32[2,160,128]{2,1,0:T(8,128)S(1)}, f32[2,160,128]{2,1,0:T(8,128)S(1)}, f32[8,128]{1,0:T(8,128)S(1)}, ...) custom-call(s32[1,1]{1,0:T(1,128)S(6)} %copy.20.counts, ...), custom_call_target="tpu_custom_call" | custom-call | tf_op jit(solution)/shard_map/pallas_call | solution.py:703
  15.6 0.0 copy-done.5
  15.6 0.0 copy-done.4
  15.6 6.5 %shard_map.176 = (f32[2,2,160,128]{3,2,1,0:T(8,128)S(1)}, f32[8,32,128]{2,1,0:T(8,128)S(1)}, f32[2,160,128]{2,1,0:T(8,128)}) custom-call(s32[1,1]{1,0:T(1,128)S(6)} %copy.20.counts, s32[1,1,16]{2,1,0:T(1,128)S(1)} %copy-done.4, s32[1,1,16]{2,1,0:T(1,128)S(1)} %copy-done.5, f32[2,2,160,128]{3,2,1,0:T(8,128)S(1)} %get-tuple-element.30.ext.ext0, ...), custom_call_target="tpu_custom_call" | custom-call | tf_op jit(solution)/shard_map/pallas_call | solution.py:716
  22.1 0.0 copy-start.1
  22.1 0.0 copy-start.3
  22.1 19.0 %shard_map.177 = (f32[2,2,160,128]{3,2,1,0:T(8,128)S(1)}, f32[2,128,128]{2,1,0:T(8,128)S(1)}, f32[8,128]{1,0:T(8,128)S(1)}) custom-call(f32[2,2,160,128]{3,2,1,0:T(8,128)S(1)} %get-tuple-element.37.grad, f32[8,32,128]{2,1,0:T(8,128)S(1)} %get-tuple-element.38.parts, f32[2,160,128]{2,1,0:T(8,128)S(1)} %get-tuple-element.39.packs, ...), custom_call_target="tpu_custom_call" | custom-call | tf_op jit(solution)/shard_map/pallas_call | solution.py:721
  41.1 0.0 copy-start
  41.1 0.0 copy-start.2
  41.2 5.8 %shard_map.178 = (f32[2,2,160,128]{3,2,1,0:T(8,128)S(1)}, f32[8,32,128]{2,1,0:T(8,128)S(1)}, f32[2,160,128]{2,1,0:T(8,128)S(1)}) custom-call(s32[1,1]{1,0:T(1,128)S(6)} %copy.20.counts, s32[1,1,16]{2,1,0:T(1,128)S(1)} %copy-done.4, s32[1,1,16]{2,1,0:T(1,128)S(1)} %copy-done.5, f32[2,2,160,128]{3,2,1,0:T(8,128)S(1)} %get-tuple-element.42.ext, ...), custom_call_target="tpu_custom_call" | custom-call | tf_op jit(solution)/shard_map/pallas_call | solution.py:716
  46.9 0.0 copy-done.1
  47.0 0.0 copy-done.3
  47.0 22.7 %shard_map.179 = (f32[2,160,128]{2,1,0:T(8,128)S(1)}, f32[8,10,16,256]{3,2,1,0:T(8,128)S(1)}, f32[8,32,128]{2,1,0:T(8,128)S(1)}, f32[8,12,16,128]{3,2,1,0:T(8,12...) custom-call(f32[2,2,160,128]{3,2,1,0:T(8,128)S(1)} %get-tuple-element.42.ext, ...), custom_call_target="tpu_custom_call" | custom-call | tf_op jit(solution)/shard_map/pallas_call | solution.py:735
  69.7 0.0 copy-done
  69.7 0.0 copy-done.2
  69.7 9.2 %shard_map.180 = (bf16[2,10,32,2048]{3,2,1,0:T(8,128)(2,1)}, f32[2,128,128]{2,1,0:T(8,128)}, f32[2,160,128]{2,1,0:T(8,128)}) custom-call(f32[8,10,16,256]{3,2,1,0:T(8,128)S(1)} %get-tuple-element.47.rows, f32[8,12,16,128]{3,2,1,0:T(8,128)S(1)} %get-tuple-element.48.bases, f32[8,16,16,128]{3,2,1,0:T(8,128)S(1)} %get-tuple-element.49.cosines, ...), custom_call_target="tpu_custom_call" | custom-call | tf_op jit(solution)/shard_map/pallas_call | solution.py:749
Async XLA Ops:
  0.6 15.0 %copy-start.5 = (s32[1,1,16]{2,1,0:T(1,128)S(1)}, s32[1,1,16]{2,1,0:T(1,128)}, u32[]{:S(2)}) copy-start(s32[1,1,16]{2,1,0:T(1,128)} %pos_x.3) | copy-start | bytes 196
  0.6 15.0 %copy-start.4 = (s32[1,1,16]{2,1,0:T(1,128)S(1)}, s32[1,1,16]{2,1,0:T(1,128)}, u32[]{:S(2)}) copy-start(s32[1,1,16]{2,1,0:T(1,128)} %pos_z.3) | copy-start | bytes 196
  22.1 24.9 %copy-start.1 = (bf16[768,256]{1,0:T(8,128)(2,1)S(1)}, bf16[768,256]{1,0:T(8,128)(2,1)}, u32[]{:S(2)}) copy-start(bf16[768,256]{1,0:T(8,128)(2,1)} %constant.21.clone.right_f) | copy-start | bytes 1179652
  22.1 24.9 %copy-start.3 = (f32[2,16,128]{2,1,0:T(8,128)S(1)}, f32[2,16,128]{2,1,0:T(8,128)}, u32[]{:S(2)}) copy-start(f32[2,16,128]{2,1,0:T(8,128)} %constant.20.clone.turns) | copy-start | bytes 49156
  41.1 28.6 %copy-start = (bf16[768,256]{1,0:T(8,128)(2,1)S(1)}, bf16[768,256]{1,0:T(8,128)(2,1)}, u32[]{:S(2)}) copy-start(bf16[768,256]{1,0:T(8,128)(2,1)} %constant.23.clone.right_b) | copy-start | bytes 1179652
  41.1 28.6 %copy-start.2 = (f32[2,16,128]{2,1,0:T(8,128)S(1)}, f32[2,16,128]{2,1,0:T(8,128)}, u32[]{:S(2)}) copy-start(f32[2,16,128]{2,1,0:T(8,128)} %constant.22.clone.turns) | copy-start | bytes 49156

commit v4 on v3

--- a/solution.py
+++ b/solution.py
@@ -27,6 +27,7 @@
 H = 2048
 CHUNK = 2 * PS // ANG
 GROUP = 8
+FIRST = 4
 
 F32 = jnp.float32
 BF16 = jnp.bfloat16
@@ -162,12 +163,39 @@
     return copy
 
 
+def meet_line(angle, tile):
+    barrier = pltpu.get_barrier_semaphore()
+    sides = ((tile > 0, tile - 1), (tile < TILES - 1, tile + 1))
+    for inside, peer in sides:
+
+        @pl.when(inside)
+        def _():
+            pl.semaphore_signal(barrier, inc=1, device_id=(angle, peer), device_id_type=MESH)
+
+    inner = jnp.logical_and(tile > 0, tile < TILES - 1)
+
+    @pl.when(inner)
+    def _():
+        pl.semaphore_wait(barrier, 2)
+
+    @pl.when(jnp.logical_not(inner))
+    def _():
+        pl.semaphore_wait(barrier, 1)
+
+
 def angle_peers(angle, tile):
     return [((angle + step) % ANG, tile) for step in range(1, ANG)]
 
 
+FARTHEST = sorted(range(1, TILES), key=lambda s: -(min(s // 4, 4 - s // 4) + min(s % 4, 4 - s % 4)))
+
+
+def shifted(tile, step):
+    return (tile // 4 + step // 4) % 4 * 4 + (tile % 4 + step % 4) % 4
+
+
 def tile_peers(angle, tile):
-    return [(angle, (tile + step) % TILES) for step in range(1, TILES)]
+    return [(angle, shifted(tile, step)) for step in FARTHEST]
 
 
 def neighbours(angle, tile):
@@ -241,8 +269,8 @@
 
 def start_second(source, landed, sems, angle, tile):
     return [
-        send(source, landed.at[tile], sems, step, (angle, (tile + step) % TILES))
-        for step in range(1, TILES)
+        send(source, landed.at[tile], sems, step, (angle, shifted(tile, step)))
+        for step in FARTHEST
     ]
 
 
@@ -286,7 +314,7 @@
     tables, refs = refs[:4], refs[4:]
     ext, own_target, packs, info, probe_here, data_here, *refs = refs
     tables_here, refs = refs[:4], refs[4:]
-    own, sides, from_left, from_right, block, landed, edge_sems, info_sems, local_sems = refs
+    own, sides, from_left, from_right, edge_sems, local_sems = refs
     angle, tile = place()
     fetches = [
         pltpu.make_async_copy(source, here, local_sems.at[index])
@@ -298,16 +326,13 @@
         fetch.start()
     row, lane = sublanes((8, TW)), lanes((8, TW))
     count = jnp.where((row == 0) & (lane == 0), counts[0, 0].astype(F32), 0.0)
-    block[...] = jnp.where((row == 1) & (lane == angle), shears[0], count)
+    info[...] = jnp.where((row == 1) & (lane == angle), shears[0], count)
     fetches[0].wait()
     for side, value in enumerate(packed_sides(own[0], own[1])):
         sides[side] = value
     clear_edges(from_left, from_right, tile)
-    meet(angle_peers(angle, tile) + list(neighbours(angle, tile)))
+    meet_line(angle, tile)
     edges = start_edges(sides, from_left, from_right, edge_sems, angle, tile)
-    infos = [
-        send(block, landed.at[step], info_sems, step, ((angle + step) % ANG, tile)) for step in range(1, ANG)
-    ]
     fetches[1].wait()
     for side, value in enumerate(packed_sides(own_target[0], own_target[1])):
         packs[side] = value
@@ -317,18 +342,12 @@
     for side, pair in enumerate(widened(own[0], own[1], from_left[...], from_right[...])):
         for part in range(2):
             ext[side, part] = pair[part]
-    for copy in infos:
-        copy.wait()
-    total = block[...]
-    for step in range(1, ANG):
-        total = total + landed[step]
-    info[...] = total
 
 
 def exchange_kernel(
-    grad, parts, packs, info, ext0, own_target, probe0, ext, probe, info_all,
-    from_left, from_right, goal_left, goal_right, landed_first, first_sum, landed_second, second_sum, gathered, landed_info,
-    edge_sems, goal_sems, first_sems, second_sems, third_sems, info_sems,
+    grad, parts, packs, info, ext0, own_target, probe0, ext, probe, info_some, info_all,
+    from_left, from_right, goal_left, goal_right, landed_first, first_sum, landed_second, second_sum, gathered, landed_some, landed_info,
+    edge_sems, goal_sems, first_sems, second_sems, third_sems, some_sems, info_sems,
 ):
     angle, tile = place()
     clear_edges(from_left, from_right, tile)
@@ -336,10 +355,21 @@
     meet(angle_peers(angle, tile) + tile_peers(angle, tile))
     first = start_first(parts, landed_first, first_sems, angle, tile)
     edges = start_edges(grad, from_left, from_right, edge_sems, angle, tile)
-    infos = start_second(info, landed_info, info_sems, angle, tile)
-    goals = start_edges(packs, goal_left, goal_right, goal_sems, angle, tile)
+    some = [
+        send(info, landed_some.at[step], some_sems, step, ((angle + step) % ANG, tile)) for step in range(1, ANG)
+    ]
     first_sum[...] = finish_first(first, parts, landed_first, angle)
     second = start_second(first_sum, landed_second, second_sems, angle, tile)
+    for copy in some:
+        copy.wait()
+    total = info[...]
+    for step in range(1, ANG):
+        total = total + landed_some[step]
+    info_some[...] = total
+    infos = start_second(info_some, landed_info, info_sems, angle, tile)
+    goals = start_edges(packs, goal_left, goal_right, goal_sems, angle, tile)
+    second_sum[...] = finish_second(second, first_sum, landed_second, tile)
+    third = start_third(second_sum, gathered, third_sems, angle, tile)
     finish_edges(edges, tile)
     finish_edges(goals, tile)
     low = lanes((ROWS, TW)) < HALF
@@ -352,10 +382,8 @@
             new = old - ALPHA * (total + RHO * (old - goal[side][part]))
             keep = jnp.logical_or(inside, jnp.logical_not(low) if side == 0 else low)
             ext[side, part] = jnp.where(keep, new, 0.0)
-    info_all[...] = finish_second(infos, info, landed_info, tile)
-    second_sum[...] = finish_second(second, first_sum, landed_second, tile)
-    third = start_third(second_sum, gathered, third_sems, angle, tile)
     gathered[angle] = second_sum[...]
+    info_all[...] = finish_second(infos, info_some, landed_info, tile)
     number = info_all[pl.ds(0, 1), pl.ds(0, 1)]
     for copy in third:
         copy.wait()
@@ -368,8 +396,9 @@
 def tail_kernel(
     ext, own_target, grad, rims, parts, info, turns, right_f,
     psi_new, every, gathered, bases, cosines, sines,
-    from_left, from_right, landed_first, first_sum, landed_second, second_sum, slabs, slabs_here, work, rows,
-    edge_sems, first_sems, second_sems, third_sems, slab_sems, row_sems,
+    from_left, from_right, landed_first, first_sum, landed_second, second_sum,
+    slabs_one, slabs_two, here_one, here_two, work_one, work_two, rows,
+    edge_sems, first_sems, second_sems, third_sems, one_sems, two_sems, row_sems,
 ):
     angle, tile = place()
     clear_edges(from_left, from_right, tile)
@@ -381,60 +410,89 @@
         )
         new = old - ALPHA * (total + RHO * (old - own_target[part]))
         psi_new[part] = new
-        for source, first_row in ((own_target[part] - new, part * ZS), (rims[part], (2 + part) * ZS)):
+        for source, place_at in ((own_target[part] - new, part), (rims[part], 2 + part)):
             for slab in range(TILES):
-                slabs[slab, pl.ds(first_row, ZS), :] = source[slab * ZS : (slab + 1) * ZS]
-    meet(angle_peers(angle, tile) + tile_peers(angle, tile))
-    copies = []
-    for step in range(1, TILES):
-        owner = (tile + step) % TILES
-        copies.append(send(slabs.at[owner], slabs_here.at[tile], slab_sems, step, (angle, owner)))
+                for slabs, first, count in ((slabs_one, 0, FIRST), (slabs_two, FIRST, ZS - FIRST)):
+                    start = slab * ZS + first
+                    slabs[slab, pl.ds(place_at * count, count), :] = source[start : start + count]
+    meet(tile_peers(angle, tile) + angle_peers(angle, tile))
+    halves = []
+    for slabs, landed, sems in ((slabs_one, here_one, one_sems), (slabs_two, here_two, two_sems)):
+        copies = []
+        for step in FARTHEST:
+            owner = shifted(tile, step)
+            copies.append(send(slabs.at[owner], landed.at[tile], sems, step, (angle, owner)))
+        halves.append(copies)
     first = start_first(parts, landed_first, first_sems, angle, tile)
-    edges = start_edges(rims, from_left, from_right, edge_sems, angle, tile)
-    slabs_here[tile] = slabs[tile]
-    work[...] = jnp.zeros_like(work)
+    for slabs, landed in ((slabs_one, here_one), (slabs_two, here_two)):
+        landed[tile] = slabs[tile]
+    work_one[...] = jnp.zeros_like(work_one)
+    work_two[...] = jnp.zeros_like(work_two)
     first_sum[...] = finish_first(first, parts, landed_first, angle)
     second = start_second(first_sum, landed_second, second_sems, angle, tile)
-    for copy in copies:
-        copy.wait()
-
-    low = lanes((ZS, TW)) < HALF
-    zero = jnp.zeros((ZS, TW), F32)
-    items = []
-    for index in range(TILES):
-        before = slabs_here[index - 1, pl.ds(3 * ZS, ZS), :] if index else zero
-        after = slabs_here[index + 1, pl.ds(2 * ZS, ZS), :] if index < TILES - 1 else zero
-        real = jnp.where(low, before, pltpu.roll(after, HALF, 1))
-        imag = jnp.where(low, pltpu.roll(before, HALF, 1), after)
-        items.append(
-            (
-                slabs_here[index, pl.ds(0, ZS), :] + ALPHA * real,
-                slabs_here[index, pl.ds(ZS, ZS), :] + ALPHA * imag,
+
+    def spectrum(copies, landed, work, start, count):
+        for copy in copies:
+            copy.wait()
+        low = lanes((count, TW)) < HALF
+        zero = jnp.zeros((count, TW), F32)
+        items = []
+        for index in range(TILES):
+            before = landed[index - 1, pl.ds(3 * count, count), :] if index else zero
+            after = landed[index + 1, pl.ds(2 * count, count), :] if index < TILES - 1 else zero
+            real = jnp.where(low, before, pltpu.roll(after, HALF, 1))
+            imag = jnp.where(low, pltpu.roll(before, HALF, 1), after)
+            items.append(
+                (
+                    landed[index, pl.ds(0, count), :] + ALPHA * real,
+                    landed[index, pl.ds(count, count), :] + ALPHA * imag,
+                )
             )
-        )
-    for order, item in enumerate(sixteen(items, -1)):
-        turn = (turns[0, pl.ds(order, 1), :], turns[1, pl.ds(order, 1), :])
-        real, imag = times(item, turn)
-        work[pl.ds(16 * order, ZS), pl.ds(0, TW)] = real
-        work[pl.ds(16 * order, ZS), pl.ds(TW, TW)] = imag
-    result = dot_right(work[...], right_f[...])
-    for order in range(TILES):
-        rows[:, order, :] = result[16 * order : 16 * order + ZS]
+        for order, item in enumerate(sixteen(items, -1)):
+            turn = (turns[0, pl.ds(order, 1), :], turns[1, pl.ds(order, 1), :])
+            real, imag = times(item, turn)
+            work[pl.ds(8 * order, count), pl.ds(0, TW)] = real
+            work[pl.ds(8 * order, count), pl.ds(TW, TW)] = imag
+        result = dot_right(work[...], right_f[...])
+        for order in range(TILES):
+            rows[pl.ds(start, count), order, :] = result[8 * order : 8 * order + count]
 
     chip, core = angle // 2, angle % 2
     up, down, over = (chip + 1) % 4, (chip + 3) % 4, (chip + 2) % 4
     upper, lower, across = 2 * up + core, 2 * down + core, 2 * over + core
     above, below, beside = (upper, tile), (lower, tile), (2 * chip + 1 - core, tile)
-    one, two = pl.ds(0, ZS // 2), pl.ds(ZS // 2, ZS // 2)
-    up_one = send(rows.at[one], every.at[angle, one], row_sems, 0, above)
-    down_two = send(rows.at[two], every.at[angle, two], row_sems, 1, below)
-    up_two = send(rows.at[two], every.at[angle, two], row_sems, 2, above)
-    down_one = send(rows.at[one], every.at[angle, one], row_sems, 3, below)
-    side = send(rows, every.at[angle], row_sems, 4, beside)
+    one, two = pl.ds(0, FIRST), pl.ds(FIRST, ZS - FIRST)
+    spectrum(halves[0], here_one, work_one, 0, FIRST)
+
+    def spread(part, slot):
+        peers = ((across, 0), (upper, 1), (lower, 2))
+        return [
+            send(rows.at[part], every.at[angle, part], row_sems, slot + index, (peer, tile)) for peer, index in peers
+        ]
+
+    sent_one = spread(one, 0)
+    spectrum(halves[1], here_two, work_two, FIRST, ZS - FIRST)
+    sent_two = spread(two, 3)
+    side = send(rows, every.at[angle], row_sems, 12, beside)
+    edges = start_edges(rims, from_left, from_right, edge_sems, angle, tile)
     every[angle] = rows[...]
     second_sum[...] = finish_second(second, first_sum, landed_second, tile)
-    third = start_third(second_sum, gathered, third_sems, angle, tile)
+    third = [
+        send(second_sum, gathered.at[angle], third_sems, slot, (peer, tile))
+        for slot, peer in enumerate((across, upper, lower))
+    ]
+    handed = [side, send(second_sum, gathered.at[angle], third_sems, 3, beside)]
     gathered[angle] = second_sum[...]
+    phase_tables(info, bases, cosines, sines, angle)
+
+    def hand(copies, target, sems, slot):
+        for index, source in ((1, lower), (2, upper), (0, across)):
+            copies[index].wait()
+            landed = target(source)
+            handed.append(send(landed, landed, sems, slot + index, beside))
+
+    hand(sent_one, lambda source: every.at[source, one], row_sems, 6)
+    hand(third, lambda source: gathered.at[source], third_sems, 4)
     finish_edges(edges, tile)
     for part in range(2):
         before, after = from_left[...], from_right[...]
@@ -444,29 +502,9 @@
         else:
             extra = jnp.where(low, pltpu.roll(before, HALF, 1), after)
         psi_new[part] = psi_new[part] - ALPHA * extra
-    phase_tables(info, bases, cosines, sines, angle)
-
-    def pass_on(part, slot, peer):
-        return send(every.at[part[0], part[1]], every.at[part[0], part[1]], row_sems, slot, peer)
-
-    up_one.wait_recv()
-    far_up = pass_on((lower, one), 5, above)
-    side_a = pass_on((lower, one), 6, beside)
-    down_two.wait_recv()
-    far_down = pass_on((upper, two), 7, below)
-    side_b = pass_on((upper, two), 8, beside)
-    up_two.wait_recv()
-    side_c = pass_on((lower, two), 9, beside)
-    down_one.wait_recv()
-    side_d = pass_on((upper, one), 10, beside)
-    far_up.wait_recv()
-    side_e = pass_on((across, one), 11, beside)
-    far_down.wait_recv()
-    side_f = pass_on((across, two), 12, beside)
-    for copy in (side, side_a, side_b, side_c, side_d, side_e, side_f) + tuple(third):
+    hand(sent_two, lambda source: every.at[source, two], row_sems, 9)
+    for copy in handed:
         copy.wait()
-    for copy in (up_one, down_two, up_two, down_one, far_up, far_down):
-        copy.wait_send()
 
 
 def gradient_kernel(
@@ -706,8 +744,8 @@
         [SMEM] * 2 + [HBM] * 8,
         [VMEM] * len(outs),
         [
-            one(2, ROWS, TW), one(2, ROWS, TW), one(ROWS, TW), one(ROWS, TW), one(8, TW), one(ANG, 8, TW),
-            dma(2, 2), dma(2, ANG), dma(8),
+            one(2, ROWS, TW), one(2, ROWS, TW), one(ROWS, TW), one(ROWS, TW),
+            dma(2, 2), dma(8),
         ],
         0,
     )(counts, shears, *(pltpu.with_memory_space_constraint(x, pltpu.HBM) for x in (psi, target, probe, data, *tables)))
@@ -718,15 +756,15 @@
         )(counts, pos_z, pos_x, ext, probe, data, *tables)
 
     grad, parts, rims = gradient(ext, probe)
-    ext, probe, info_all = call(
+    ext, probe, info, info_all = call(
         exchange_kernel,
-        [wide, square, small],
+        [wide, square, small, small],
         [VMEM] * 7,
-        [VMEM] * 3,
+        [VMEM] * 4,
         [
             one(2, ROWS, TW), one(2, ROWS, TW), one(ROWS, TW), one(ROWS, TW),
-            one(ANG, CHUNK, TW), one(CHUNK, TW), one(TILES, CHUNK, TW), one(CHUNK, TW), one(ANG, CHUNK, TW), one(TILES, 8, TW),
-            dma(2, 2), dma(2, 2), dma(2, ANG), dma(2, TILES), dma(2, ANG), dma(2, TILES),
+            one(ANG, CHUNK, TW), one(CHUNK, TW), one(TILES, CHUNK, TW), one(CHUNK, TW), one(ANG, CHUNK, TW), one(ANG, 8, TW), one(TILES, 8, TW),
+            dma(2, 2), dma(2, 2), dma(2, ANG), dma(2, TILES), dma(2, ANG), dma(2, ANG), dma(2, TILES),
         ],
         1,
     )(grad, parts, packs, info, ext, goal, probe)
@@ -740,8 +778,10 @@
         [
             one(ROWS, TW), one(ROWS, TW),
             one(ANG, CHUNK, TW), one(CHUNK, TW), one(TILES, CHUNK, TW), one(CHUNK, TW),
-            one(TILES, 4 * ZS, TW), one(TILES, 4 * ZS, TW), one(WIDE, WIDE), one(ZS, TILES, WIDE),
-            dma(2, 2), dma(2, ANG), dma(2, TILES), dma(2, ANG), dma(2, TILES), dma(2, 13),
+            one(TILES, 4 * FIRST, TW), one(TILES, 4 * (ZS - FIRST), TW),
+            one(TILES, 4 * FIRST, TW), one(TILES, 4 * (ZS - FIRST), TW),
+            one(PS, WIDE), one(PS, WIDE), one(ZS, TILES, WIDE),
+            dma(2, 2), dma(2, ANG), dma(2, TILES), dma(2, ANG), dma(2, TILES), dma(2, TILES), dma(2, 13),
         ],
         2,
     )(ext, goal, grad, rims, parts, info, jnp.asarray(turn_table(-1)), jnp.asarray(right_table(dft_block(TW, 1.0))))

time: 78.4 us -> 75.2 us (0.959); the launches traced: 78.9 us -> 74.6 us
  Pallas kernels: 76.8 us -> 72.5 us
    pallas_call x1, Pallas kernels: 13.6 us -> 6.43 us  [shards(): call(halo_kernel, outs, [SMEM] * 2 + [HBM] * 8, [VMEM] * len(outs), [one(...]
    pallas_call x1, Pallas kernels: 19 us -> 26 us  [shards(): call(exchange_kernel, [wide, square, small, small], [VMEM] * 7, [VMEM] *...]
    pallas_call x2, Pallas kernels: 12.2 us -> 7.1 us  [gradient(): call(gradient_kernel, [wide, chunks, edge], [SMEM] * 3 + [VMEM] * 7, [VME...]
    pallas_call x1, Pallas kernels: 22.7 us -> 23.8 us  [shards(): call(tail_kernel, [edge, every, chunks, arr(ANG, 12, TILES, TW), phases,...]
where the time goes in v4:
time: 75.2 us; the launch traced here: 74.6 us
  Pallas kernels  72.5 us (96%)
  between operations  2.05 us (3%)
    pallas_call x1, Pallas kernels, shards(): call(exchange_kernel, [wide, square, small, small], [VMEM] * 7, [VMEM] *...  26 us
    pallas_call x1, Pallas kernels, shards(): call(tail_kernel, [edge, every, chunks, arr(ANG, 12, TILES, TW), phases,...  23.8 us
    pallas_call x1, Pallas kernels, shards(): call(image_kernel, [jax.ShapeDtypeStruct((2, ZS, YB, H), BF16), square, e...  9.16 us
    pallas_call x2, Pallas kernels, gradient(): call(gradient_kernel, [wide, chunks, edge], [SMEM] * 3 + [VMEM] * 7, [VME...  7.1 us
    pallas_call x1, Pallas kernels, shards(): call(halo_kernel, outs, [SMEM] * 2 + [HBM] * 8, [VMEM] * len(outs), [one(...  6.43 us

profile of v4, /device:TPU:1, one launch (start us, length us, event | category | flops | bytes accessed | tf_op | source)
XLA Modules:
  0.0 74.6 jit_solution(11315730477573035437)
XLA Ops:
  0.6 0.0 copy-start.5
  0.6 0.0 copy-start.4
  2.0 6.4 %shard_map.175 = (f32[2,2,160,128]{3,2,1,0:T(8,128)S(1)}, f32[2,160,128]{2,1,0:T(8,128)S(1)}, f32[2,160,128]{2,1,0:T(8,128)S(1)}, f32[8,128]{1,0:T(8,128)S(1)}, ...) custom-call(s32[1,1]{1,0:T(1,128)S(6)} %copy.20.counts, ...), custom_call_target="tpu_custom_call" | custom-call | tf_op jit(solution)/shard_map/pallas_call | solution.py:741
  8.4 0.0 copy-done.5
  8.4 0.0 copy-done.4
  8.4 3.9 %shard_map.176 = (f32[2,2,160,128]{3,2,1,0:T(8,128)S(1)}, f32[8,32,128]{2,1,0:T(8,128)S(1)}, f32[2,160,128]{2,1,0:T(8,128)}) custom-call(s32[1,1]{1,0:T(1,128)S(6)} %copy.20.counts, s32[1,1,16]{2,1,0:T(1,128)S(1)} %copy-done.4, s32[1,1,16]{2,1,0:T(1,128)S(1)} %copy-done.5, f32[2,2,160,128]{3,2,1,0:T(8,128)S(1)} %get-tuple-element.31.ext.ext0, ...), custom_call_target="tpu_custom_call" | custom-call | tf_op jit(solution)/shard_map/pallas_call | solution.py:754
  12.3 0.0 copy-start.1
  12.3 0.0 copy-start.3
  12.3 26.0 %shard_map.177 = (f32[2,2,160,128]{3,2,1,0:T(8,128)S(1)}, f32[2,128,128]{2,1,0:T(8,128)S(1)}, f32[8,128]{1,0:T(8,128)S(1)}, f32[8,128]{1,0:T(8,128)S(1)}) custom-call(f32[2,2,160,128]{3,2,1,0:T(8,128)S(1)} %get-tuple-element.38.grad, f32[8,32,128]{2,1,0:T(8,128)S(1)} %get-tuple-element.39.parts, f32[2,160,128]{2,1,0:T(8,128)S(1)} %get-tuple-element.40.packs, ...), custom_call_target="tpu_custom_call" | custom-call | tf_op jit(solution)/shard_map/pallas_call | solution.py:759
  38.3 0.0 copy-start
  38.3 0.0 copy-start.2
  38.4 3.2 %shard_map.178 = (f32[2,2,160,128]{3,2,1,0:T(8,128)S(1)}, f32[8,32,128]{2,1,0:T(8,128)S(1)}, f32[2,160,128]{2,1,0:T(8,128)S(1)}) custom-call(s32[1,1]{1,0:T(1,128)S(6)} %copy.20.counts, s32[1,1,16]{2,1,0:T(1,128)S(1)} %copy-done.4, s32[1,1,16]{2,1,0:T(1,128)S(1)} %copy-done.5, f32[2,2,160,128]{3,2,1,0:T(8,128)S(1)} %get-tuple-element.43.ext, ...), custom_call_target="tpu_custom_call" | custom-call | tf_op jit(solution)/shard_map/pallas_call | solution.py:754
  41.6 0.0 copy-done.1
  41.6 0.0 copy-done.3
  41.6 23.8 %shard_map.179 = (f32[2,160,128]{2,1,0:T(8,128)S(1)}, f32[8,10,16,256]{3,2,1,0:T(8,128)S(1)}, f32[8,32,128]{2,1,0:T(8,128)S(1)}, f32[8,12,16,128]{3,2,1,0:T(8,12...) custom-call(f32[2,2,160,128]{3,2,1,0:T(8,128)S(1)} %get-tuple-element.43.ext, ...), custom_call_target="tpu_custom_call" | custom-call | tf_op jit(solution)/shard_map/pallas_call | solution.py:773
  65.4 0.0 copy-done
  65.4 0.0 copy-done.2
  65.4 9.2 %shard_map.180 = (bf16[2,10,32,2048]{3,2,1,0:T(8,128)(2,1)}, f32[2,128,128]{2,1,0:T(8,128)}, f32[2,160,128]{2,1,0:T(8,128)}) custom-call(f32[8,10,16,256]{3,2,1,0:T(8,128)S(1)} %get-tuple-element.49.rows, f32[8,12,16,128]{3,2,1,0:T(8,128)S(1)} %get-tuple-element.50.bases, f32[8,16,16,128]{3,2,1,0:T(8,128)S(1)} %get-tuple-element.51.cosines, ...), custom_call_target="tpu_custom_call" | custom-call | tf_op jit(solution)/shard_map/pallas_call | solution.py:789
Async XLA Ops:
  0.6 7.8 %copy-start.5 = (s32[1,1,16]{2,1,0:T(1,128)S(1)}, s32[1,1,16]{2,1,0:T(1,128)}, u32[]{:S(2)}) copy-start(s32[1,1,16]{2,1,0:T(1,128)} %pos_x.3) | copy-start | bytes 196
  0.6 7.8 %copy-start.4 = (s32[1,1,16]{2,1,0:T(1,128)S(1)}, s32[1,1,16]{2,1,0:T(1,128)}, u32[]{:S(2)}) copy-start(s32[1,1,16]{2,1,0:T(1,128)} %pos_z.3) | copy-start | bytes 196
  12.3 29.2 %copy-start.1 = (bf16[768,256]{1,0:T(8,128)(2,1)S(1)}, bf16[768,256]{1,0:T(8,128)(2,1)}, u32[]{:S(2)}) copy-start(bf16[768,256]{1,0:T(8,128)(2,1)} %constant.21.clone.right_f) | copy-start | bytes 1179652
  12.3 29.3 %copy-start.3 = (f32[2,16,128]{2,1,0:T(8,128)S(1)}, f32[2,16,128]{2,1,0:T(8,128)}, u32[]{:S(2)}) copy-start(f32[2,16,128]{2,1,0:T(8,128)} %constant.20.clone.turns) | copy-start | bytes 49156
  38.3 27.1 %copy-start = (bf16[768,256]{1,0:T(8,128)(2,1)S(1)}, bf16[768,256]{1,0:T(8,128)(2,1)}, u32[]{:S(2)}) copy-start(bf16[768,256]{1,0:T(8,128)(2,1)} %constant.23.clone.right_b) | copy-start | bytes 1179652
  38.3 27.1 %copy-start.2 = (f32[2,16,128]{2,1,0:T(8,128)S(1)}, f32[2,16,128]{2,1,0:T(8,128)}, u32[]{:S(2)}) copy-start(f32[2,16,128]{2,1,0:T(8,128)} %constant.22.clone.turns) | copy-start | bytes 49156

commit v5 on v4

--- a/solution.py
+++ b/solution.py
@@ -143,11 +143,11 @@
     return lax.axis_index("angle"), lax.axis_index("tile")
 
 
-def meet(peers):
+def greet(peers):
     barrier = pltpu.get_barrier_semaphore()
     for peer in peers:
         pl.semaphore_signal(barrier, inc=1, device_id=peer, device_id_type=MESH)
-    pl.semaphore_wait(barrier, len(peers))
+    return lambda: pl.semaphore_wait(barrier, len(peers))
 
 
 def send(source, target, sems, slot, peer):
@@ -163,7 +163,7 @@
     return copy
 
 
-def meet_line(angle, tile):
+def greet_line(angle, tile):
     barrier = pltpu.get_barrier_semaphore()
     sides = ((tile > 0, tile - 1), (tile < TILES - 1, tile + 1))
     for inside, peer in sides:
@@ -174,13 +174,16 @@
 
     inner = jnp.logical_and(tile > 0, tile < TILES - 1)
 
-    @pl.when(inner)
-    def _():
-        pl.semaphore_wait(barrier, 2)
-
-    @pl.when(jnp.logical_not(inner))
-    def _():
-        pl.semaphore_wait(barrier, 1)
+    def wait():
+        @pl.when(inner)
+        def _():
+            pl.semaphore_wait(barrier, 2)
+
+        @pl.when(jnp.logical_not(inner))
+        def _():
+            pl.semaphore_wait(barrier, 1)
+
+    return wait
 
 
 def angle_peers(angle, tile):
@@ -324,14 +327,15 @@
     ]
     for fetch in fetches:
         fetch.start()
+    clear_edges(from_left, from_right, tile)
+    met = greet_line(angle, tile)
     row, lane = sublanes((8, TW)), lanes((8, TW))
     count = jnp.where((row == 0) & (lane == 0), counts[0, 0].astype(F32), 0.0)
     info[...] = jnp.where((row == 1) & (lane == angle), shears[0], count)
     fetches[0].wait()
     for side, value in enumerate(packed_sides(own[0], own[1])):
         sides[side] = value
-    clear_edges(from_left, from_right, tile)
-    meet_line(angle, tile)
+    met()
     edges = start_edges(sides, from_left, from_right, edge_sems, angle, tile)
     fetches[1].wait()
     for side, value in enumerate(packed_sides(own_target[0], own_target[1])):
@@ -352,7 +356,7 @@
     angle, tile = place()
     clear_edges(from_left, from_right, tile)
     clear_edges(goal_left, goal_right, tile)
-    meet(angle_peers(angle, tile) + tile_peers(angle, tile))
+    greet(tile_peers(angle, tile) + angle_peers(angle, tile))()
     first = start_first(parts, landed_first, first_sems, angle, tile)
     edges = start_edges(grad, from_left, from_right, edge_sems, angle, tile)
     some = [
@@ -402,6 +406,7 @@
 ):
     angle, tile = place()
     clear_edges(from_left, from_right, tile)
+    met = greet(tile_peers(angle, tile) + angle_peers(angle, tile))
     low = lanes((ROWS, TW)) < HALF
     for part in range(2):
         old, total = (
@@ -415,7 +420,9 @@
                 for slabs, first, count in ((slabs_one, 0, FIRST), (slabs_two, FIRST, ZS - FIRST)):
                     start = slab * ZS + first
                     slabs[slab, pl.ds(place_at * count, count), :] = source[start : start + count]
-    meet(tile_peers(angle, tile) + angle_peers(angle, tile))
+    work_one[...] = jnp.zeros_like(work_one)
+    work_two[...] = jnp.zeros_like(work_two)
+    met()
     halves = []
     for slabs, landed, sems in ((slabs_one, here_one, one_sems), (slabs_two, here_two, two_sems)):
         copies = []
@@ -426,8 +433,6 @@
     first = start_first(parts, landed_first, first_sems, angle, tile)
     for slabs, landed in ((slabs_one, here_one), (slabs_two, here_two)):
         landed[tile] = slabs[tile]
-    work_one[...] = jnp.zeros_like(work_one)
-    work_two[...] = jnp.zeros_like(work_two)
     first_sum[...] = finish_first(first, parts, landed_first, angle)
     second = start_second(first_sum, landed_second, second_sems, angle, tile)
 
@@ -535,7 +540,8 @@
             rows.append(sheet(times((probe_real, probe_imag), (real, imag)), 1))
         pairs = range(0, GROUP, 2)
         sides = (slice(0, PS), slice(PS, 2 * PS))
-        turned = [dot_right(sheet(rows[p : p + 2], 0), right_f[...]) for p in pairs]
+        turned = [dot_right(sheet(rows[p : p + 4], 0), right_f[...]) for p in range(0, GROUP, 4)]
+        turned = [v[k] for v in turned for k in (slice(0, 2 * PS), slice(2 * PS, 4 * PS))]
         turned = [sheet([sheet([v[k, :PS], v[k, PS:]], 0) for k in sides], 1) for v in turned]
         far = [dot_left(left_f[...], v) for v in turned]
         weighted = []
@@ -547,7 +553,8 @@
             weighted.append(sheet([misfit * far_real, misfit * far_imag], 0))
         turned = [dot_left(left_b[...], sheet(weighted[p : p + 2], 1)) for p in pairs]
         turned = [sheet([sheet([v[:PS, k], v[PS:, k]], 1) for k in sides], 0) for v in turned]
-        chi = [dot_right(v, right_b[...]) for v in turned]
+        chi = [dot_right(sheet(turned[p : p + 2], 0), right_b[...]) for p in range(0, GROUP // 2, 2)]
+        chi = [v[k] for v in chi for k in (slice(0, 2 * PS), slice(2 * PS, 4 * PS))]
         for s in range(GROUP):
             slot, start_z, start_x = spots[s]
             here = pl.ds(start_z, PS)

time: 75.2 us -> 73.3 us (0.975)
  Pallas kernels: 72.5 us -> 71.1 us
    pallas_call x1, Pallas kernels: 6.43 us -> 5.42 us  [shards(): call(halo_kernel, outs, [SMEM] * 2 + [HBM] * 8, [VMEM] * len(outs), [one(...]
where the time goes in v5:
time: 73.3 us; the launch traced here: 73.2 us
  Pallas kernels  71.1 us (97%)
  between operations  2.05 us (3%)
    pallas_call x1, Pallas kernels, shards(): call(exchange_kernel, [wide, square, small, small], [VMEM] * 7, [VMEM] *...  25.8 us
    pallas_call x1, Pallas kernels, shards(): call(tail_kernel, [edge, every, chunks, arr(ANG, 12, TILES, TW), phases,...  23.8 us
    pallas_call x1, Pallas kernels, shards(): call(image_kernel, [jax.ShapeDtypeStruct((2, ZS, YB, H), BF16), square, e...  9.16 us
    pallas_call x2, Pallas kernels, gradient(): call(gradient_kernel, [wide, chunks, edge], [SMEM] * 3 + [VMEM] * 7, [VME...  7.03 us
    pallas_call x1, Pallas kernels, shards(): call(halo_kernel, outs, [SMEM] * 2 + [HBM] * 8, [VMEM] * len(outs), [one(...  5.42 us

profile of v5, /device:TPU:1, one launch (start us, length us, event | category | flops | bytes accessed | tf_op | source)
XLA Modules:
  0.0 73.2 jit_solution(5387344344220430387)
XLA Ops:
  0.6 0.0 copy-start.5
  0.6 0.0 copy-start.4
  2.0 5.4 %shard_map.175 = (f32[2,2,160,128]{3,2,1,0:T(8,128)S(1)}, f32[2,160,128]{2,1,0:T(8,128)S(1)}, f32[2,160,128]{2,1,0:T(8,128)S(1)}, f32[8,128]{1,0:T(8,128)S(1)}, ...) custom-call(s32[1,1]{1,0:T(1,128)S(6)} %copy.20.counts, ...), custom_call_target="tpu_custom_call" | custom-call | tf_op jit(solution)/shard_map/pallas_call | solution.py:748
  7.4 0.0 copy-done.5
  7.4 0.0 copy-done.4
  7.4 3.9 %shard_map.176 = (f32[2,2,160,128]{3,2,1,0:T(8,128)S(1)}, f32[8,32,128]{2,1,0:T(8,128)S(1)}, f32[2,160,128]{2,1,0:T(8,128)}) custom-call(s32[1,1]{1,0:T(1,128)S(6)} %copy.20.counts, s32[1,1,16]{2,1,0:T(1,128)S(1)} %copy-done.4, s32[1,1,16]{2,1,0:T(1,128)S(1)} %copy-done.5, f32[2,2,160,128]{3,2,1,0:T(8,128)S(1)} %get-tuple-element.31.ext.ext0, ...), custom_call_target="tpu_custom_call" | custom-call | tf_op jit(solution)/shard_map/pallas_call | solution.py:761
  11.3 0.0 copy-start.1
  11.3 0.0 copy-start.3
  11.3 25.8 %shard_map.177 = (f32[2,2,160,128]{3,2,1,0:T(8,128)S(1)}, f32[2,128,128]{2,1,0:T(8,128)S(1)}, f32[8,128]{1,0:T(8,128)S(1)}, f32[8,128]{1,0:T(8,128)S(1)}) custom-call(f32[2,2,160,128]{3,2,1,0:T(8,128)S(1)} %get-tuple-element.38.grad, f32[8,32,128]{2,1,0:T(8,128)S(1)} %get-tuple-element.39.parts, f32[2,160,128]{2,1,0:T(8,128)S(1)} %get-tuple-element.40.packs, ...), custom_call_target="tpu_custom_call" | custom-call | tf_op jit(solution)/shard_map/pallas_call | solution.py:766
  37.1 0.0 copy-start
  37.1 0.0 copy-start.2
  37.1 3.2 %shard_map.178 = (f32[2,2,160,128]{3,2,1,0:T(8,128)S(1)}, f32[8,32,128]{2,1,0:T(8,128)S(1)}, f32[2,160,128]{2,1,0:T(8,128)S(1)}) custom-call(s32[1,1]{1,0:T(1,128)S(6)} %copy.20.counts, s32[1,1,16]{2,1,0:T(1,128)S(1)} %copy-done.4, s32[1,1,16]{2,1,0:T(1,128)S(1)} %copy-done.5, f32[2,2,160,128]{3,2,1,0:T(8,128)S(1)} %get-tuple-element.43.ext, ...), custom_call_target="tpu_custom_call" | custom-call | tf_op jit(solution)/shard_map/pallas_call | solution.py:761
  40.2 0.0 copy-done.1
  40.3 0.0 copy-done.3
  40.3 23.8 %shard_map.179 = (f32[2,160,128]{2,1,0:T(8,128)S(1)}, f32[8,10,16,256]{3,2,1,0:T(8,128)S(1)}, f32[8,32,128]{2,1,0:T(8,128)S(1)}, f32[8,12,16,128]{3,2,1,0:T(8,12...) custom-call(f32[2,2,160,128]{3,2,1,0:T(8,128)S(1)} %get-tuple-element.43.ext, ...), custom_call_target="tpu_custom_call" | custom-call | tf_op jit(solution)/shard_map/pallas_call | solution.py:780
  64.1 0.0 copy-done
  64.1 0.0 copy-done.2
  64.1 9.2 %shard_map.180 = (bf16[2,10,32,2048]{3,2,1,0:T(8,128)(2,1)}, f32[2,128,128]{2,1,0:T(8,128)}, f32[2,160,128]{2,1,0:T(8,128)}) custom-call(f32[8,10,16,256]{3,2,1,0:T(8,128)S(1)} %get-tuple-element.49.rows, f32[8,12,16,128]{3,2,1,0:T(8,128)S(1)} %get-tuple-element.50.bases, f32[8,16,16,128]{3,2,1,0:T(8,128)S(1)} %get-tuple-element.51.cosines, ...), custom_call_target="tpu_custom_call" | custom-call | tf_op jit(solution)/shard_map/pallas_call | solution.py:796
Async XLA Ops:
  0.6 6.8 %copy-start.5 = (s32[1,1,16]{2,1,0:T(1,128)S(1)}, s32[1,1,16]{2,1,0:T(1,128)}, u32[]{:S(2)}) copy-start(s32[1,1,16]{2,1,0:T(1,128)} %pos_x.3) | copy-start | bytes 196
  0.6 6.8 %copy-start.4 = (s32[1,1,16]{2,1,0:T(1,128)S(1)}, s32[1,1,16]{2,1,0:T(1,128)}, u32[]{:S(2)}) copy-start(s32[1,1,16]{2,1,0:T(1,128)} %pos_z.3) | copy-start | bytes 196
  11.3 29.0 %copy-start.1 = (bf16[768,256]{1,0:T(8,128)(2,1)S(1)}, bf16[768,256]{1,0:T(8,128)(2,1)}, u32[]{:S(2)}) copy-start(bf16[768,256]{1,0:T(8,128)(2,1)} %constant.21.clone.right_f) | copy-start | bytes 1179652
  11.3 29.0 %copy-start.3 = (f32[2,16,128]{2,1,0:T(8,128)S(1)}, f32[2,16,128]{2,1,0:T(8,128)}, u32[]{:S(2)}) copy-start(f32[2,16,128]{2,1,0:T(8,128)} %constant.20.clone.turns) | copy-start | bytes 49156
  37.1 27.0 %copy-start = (bf16[768,256]{1,0:T(8,128)(2,1)S(1)}, bf16[768,256]{1,0:T(8,128)(2,1)}, u32[]{:S(2)}) copy-start(bf16[768,256]{1,0:T(8,128)(2,1)} %constant.23.clone.right_b) | copy-start | bytes 1179652
  37.1 27.0 %copy-start.2 = (f32[2,16,128]{2,1,0:T(8,128)S(1)}, f32[2,16,128]{2,1,0:T(8,128)}, u32[]{:S(2)}) copy-start(f32[2,16,128]{2,1,0:T(8,128)} %constant.22.clone.turns) | copy-start | bytes 49156

commit v6 on v5

--- a/solution.py
+++ b/solution.py
@@ -186,8 +186,11 @@
     return wait
 
 
+OPPOSITE = (4, 3, 5, 2, 6, 1, 7)
+
+
 def angle_peers(angle, tile):
-    return [((angle + step) % ANG, tile) for step in range(1, ANG)]
+    return [((angle + step) % ANG, tile) for step in OPPOSITE]
 
 
 FARTHEST = sorted(range(1, TILES), key=lambda s: -(min(s // 4, 4 - s // 4) + min(s % 4, 4 - s % 4)))
@@ -257,7 +260,7 @@
 def start_first(parts, landed, sems, angle, tile):
     return [
         send(parts.at[(angle + step) % ANG], landed.at[step], sems, step, ((angle + step) % ANG, tile))
-        for step in range(1, ANG)
+        for step in OPPOSITE
     ]
 
 
@@ -290,7 +293,7 @@
 def start_third(source, gathered, sems, angle, tile):
     return [
         send(source, gathered.at[angle], sems, step, ((angle + step) % ANG, tile))
-        for step in range(1, ANG)
+        for step in OPPOSITE
     ]
 
 
@@ -360,7 +363,7 @@
     first = start_first(parts, landed_first, first_sems, angle, tile)
     edges = start_edges(grad, from_left, from_right, edge_sems, angle, tile)
     some = [
-        send(info, landed_some.at[step], some_sems, step, ((angle + step) % ANG, tile)) for step in range(1, ANG)
+        send(info, landed_some.at[step], some_sems, step, ((angle + step) % ANG, tile)) for step in OPPOSITE
     ]
     first_sum[...] = finish_first(first, parts, landed_first, angle)
     second = start_second(first_sum, landed_second, second_sems, angle, tile)

time: 73.3 us -> 73.6 us (level)
  Pallas kernels: 71.1 us -> 72 us
    pallas_call x1, Pallas kernels: 23.8 us -> 24.6 us  [shards(): call(tail_kernel, [edge, every, chunks, arr(ANG, 12, TILES, TW), phases,...]
where the time goes in v6:
time: 73.6 us; the launch traced here: 74.1 us
  Pallas kernels  72 us (98%)
  between operations  2.05 us (3%)
    pallas_call x1, Pallas kernels, shards(): call(exchange_kernel, [wide, square, small, small], [VMEM] * 7, [VMEM] *...  25.8 us
    pallas_call x1, Pallas kernels, shards(): call(tail_kernel, [edge, every, chunks, arr(ANG, 12, TILES, TW), phases,...  24.6 us
    pallas_call x1, Pallas kernels, shards(): call(image_kernel, [jax.ShapeDtypeStruct((2, ZS, YB, H), BF16), square, e...  9.16 us
    pallas_call x2, Pallas kernels, gradient(): call(gradient_kernel, [wide, chunks, edge], [SMEM] * 3 + [VMEM] * 7, [VME...  7.03 us
    pallas_call x1, Pallas kernels, shards(): call(halo_kernel, outs, [SMEM] * 2 + [HBM] * 8, [VMEM] * len(outs), [one(...  5.42 us

profile of v6, /device:TPU:1, one launch (start us, length us, event | category | flops | bytes accessed | tf_op | source)
XLA Modules:
  0.0 74.1 jit_solution(3518163807751716724)
XLA Ops:
  0.6 0.0 copy-start.5
  0.6 0.0 copy-start.4
  2.0 5.4 %shard_map.175 = (f32[2,2,160,128]{3,2,1,0:T(8,128)S(1)}, f32[2,160,128]{2,1,0:T(8,128)S(1)}, f32[2,160,128]{2,1,0:T(8,128)S(1)}, f32[8,128]{1,0:T(8,128)S(1)}, ...) custom-call(s32[1,1]{1,0:T(1,128)S(6)} %copy.20.counts, ...), custom_call_target="tpu_custom_call" | custom-call | tf_op jit(solution)/shard_map/pallas_call | solution.py:751
  7.4 0.0 copy-done.5
  7.4 0.0 copy-done.4
  7.4 3.9 %shard_map.176 = (f32[2,2,160,128]{3,2,1,0:T(8,128)S(1)}, f32[8,32,128]{2,1,0:T(8,128)S(1)}, f32[2,160,128]{2,1,0:T(8,128)}) custom-call(s32[1,1]{1,0:T(1,128)S(6)} %copy.20.counts, s32[1,1,16]{2,1,0:T(1,128)S(1)} %copy-done.4, s32[1,1,16]{2,1,0:T(1,128)S(1)} %copy-done.5, f32[2,2,160,128]{3,2,1,0:T(8,128)S(1)} %get-tuple-element.31.ext.ext0, ...), custom_call_target="tpu_custom_call" | custom-call | tf_op jit(solution)/shard_map/pallas_call | solution.py:764
  11.3 0.0 copy-start.1
  11.3 0.0 copy-start.3
  11.3 25.8 %shard_map.177 = (f32[2,2,160,128]{3,2,1,0:T(8,128)S(1)}, f32[2,128,128]{2,1,0:T(8,128)S(1)}, f32[8,128]{1,0:T(8,128)S(1)}, f32[8,128]{1,0:T(8,128)S(1)}) custom-call(f32[2,2,160,128]{3,2,1,0:T(8,128)S(1)} %get-tuple-element.38.grad, f32[8,32,128]{2,1,0:T(8,128)S(1)} %get-tuple-element.39.parts, f32[2,160,128]{2,1,0:T(8,128)S(1)} %get-tuple-element.40.packs, ...), custom_call_target="tpu_custom_call" | custom-call | tf_op jit(solution)/shard_map/pallas_call | solution.py:769
  37.1 0.0 copy-start
  37.1 0.0 copy-start.2
  37.2 3.2 %shard_map.178 = (f32[2,2,160,128]{3,2,1,0:T(8,128)S(1)}, f32[8,32,128]{2,1,0:T(8,128)S(1)}, f32[2,160,128]{2,1,0:T(8,128)S(1)}) custom-call(s32[1,1]{1,0:T(1,128)S(6)} %copy.20.counts, s32[1,1,16]{2,1,0:T(1,128)S(1)} %copy-done.4, s32[1,1,16]{2,1,0:T(1,128)S(1)} %copy-done.5, f32[2,2,160,128]{3,2,1,0:T(8,128)S(1)} %get-tuple-element.43.ext, ...), custom_call_target="tpu_custom_call" | custom-call | tf_op jit(solution)/shard_map/pallas_call | solution.py:764
  40.3 0.0 copy-done.1
  40.3 0.0 copy-done.3
  40.3 24.6 %shard_map.179 = (f32[2,160,128]{2,1,0:T(8,128)S(1)}, f32[8,10,16,256]{3,2,1,0:T(8,128)S(1)}, f32[8,32,128]{2,1,0:T(8,128)S(1)}, f32[8,12,16,128]{3,2,1,0:T(8,12...) custom-call(f32[2,2,160,128]{3,2,1,0:T(8,128)S(1)} %get-tuple-element.43.ext, ...), custom_call_target="tpu_custom_call" | custom-call | tf_op jit(solution)/shard_map/pallas_call | solution.py:783
  65.0 0.0 copy-done
  65.0 0.0 copy-done.2
  65.0 9.2 %shard_map.180 = (bf16[2,10,32,2048]{3,2,1,0:T(8,128)(2,1)}, f32[2,128,128]{2,1,0:T(8,128)}, f32[2,160,128]{2,1,0:T(8,128)}) custom-call(f32[8,10,16,256]{3,2,1,0:T(8,128)S(1)} %get-tuple-element.49.rows, f32[8,12,16,128]{3,2,1,0:T(8,128)S(1)} %get-tuple-element.50.bases, f32[8,16,16,128]{3,2,1,0:T(8,128)S(1)} %get-tuple-element.51.cosines, ...), custom_call_target="tpu_custom_call" | custom-call | tf_op jit(solution)/shard_map/pallas_call | solution.py:799
Async XLA Ops:
  0.6 6.8 %copy-start.5 = (s32[1,1,16]{2,1,0:T(1,128)S(1)}, s32[1,1,16]{2,1,0:T(1,128)}, u32[]{:S(2)}) copy-start(s32[1,1,16]{2,1,0:T(1,128)} %pos_x.3) | copy-start | bytes 196
  0.6 6.8 %copy-start.4 = (s32[1,1,16]{2,1,0:T(1,128)S(1)}, s32[1,1,16]{2,1,0:T(1,128)}, u32[]{:S(2)}) copy-start(s32[1,1,16]{2,1,0:T(1,128)} %pos_z.3) | copy-start | bytes 196
  11.3 29.1 %copy-start.1 = (bf16[768,256]{1,0:T(8,128)(2,1)S(1)}, bf16[768,256]{1,0:T(8,128)(2,1)}, u32[]{:S(2)}) copy-start(bf16[768,256]{1,0:T(8,128)(2,1)} %constant.21.clone.right_f) | copy-start | bytes 1179652
  11.3 29.1 %copy-start.3 = (f32[2,16,128]{2,1,0:T(8,128)S(1)}, f32[2,16,128]{2,1,0:T(8,128)}, u32[]{:S(2)}) copy-start(f32[2,16,128]{2,1,0:T(8,128)} %constant.20.clone.turns) | copy-start | bytes 49156
  37.1 27.8 %copy-start = (bf16[768,256]{1,0:T(8,128)(2,1)S(1)}, bf16[768,256]{1,0:T(8,128)(2,1)}, u32[]{:S(2)}) copy-start(bf16[768,256]{1,0:T(8,128)(2,1)} %constant.23.clone.right_b) | copy-start | bytes 1179652
  37.1 27.8 %copy-start.2 = (f32[2,16,128]{2,1,0:T(8,128)S(1)}, f32[2,16,128]{2,1,0:T(8,128)}, u32[]{:S(2)}) copy-start(f32[2,16,128]{2,1,0:T(8,128)} %constant.22.clone.turns) | copy-start | bytes 49156

commit v7 on v5

--- a/solution.py
+++ b/solution.py
@@ -513,8 +513,9 @@
 
 
 def gradient_kernel(
-    counts, pos_z, pos_x, ext, probe, data, right_f, left_f, left_b, right_b, grad, parts, rims, probe_acc,
+    counts, pos_z, pos_x, ext, probe, data, right_f, left_f, left_b, right_b, grad, parts, *refs,
 ):
+    *rims, probe_acc = refs
     count = counts[0, 0]
     grad[...] = jnp.zeros_like(grad)
     probe_acc[...] = jnp.zeros_like(probe_acc)
@@ -573,9 +574,10 @@
     lax.fori_loop(0, (count + GROUP - 1) // GROUP, group, 0)
     for chunk in range(ANG):
         parts[chunk] = probe_acc[pl.ds(chunk * CHUNK, CHUNK), :]
-    low = lanes((ROWS, TW)) < HALF
-    rims[0] = jnp.where(low, grad[0, 0], pltpu.roll(grad[0, 1], HALF, 1))
-    rims[1] = jnp.where(low, pltpu.roll(grad[1, 0], HALF, 1), grad[1, 1])
+    for rim in rims:
+        low = lanes((ROWS, TW)) < HALF
+        rim[0] = jnp.where(low, grad[0, 0], pltpu.roll(grad[0, 1], HALF, 1))
+        rim[1] = jnp.where(low, pltpu.roll(grad[1, 0], HALF, 1), grad[1, 1])
 
 
 def phase_tables(info, bases, cosines, sines, here):
@@ -757,12 +759,12 @@
         0,
     )(counts, shears, *(pltpu.with_memory_space_constraint(x, pltpu.HBM) for x in (psi, target, probe, data, *tables)))
 
-    def gradient(ext, probe):
+    def gradient(ext, probe, rims):
         return call(
-            gradient_kernel, [wide, chunks, edge], [SMEM] * 3 + [VMEM] * 7, [VMEM] * 3, [one(2 * PS, PS)]
+            gradient_kernel, [wide, chunks] + rims, [SMEM] * 3 + [VMEM] * 7, [VMEM] * (2 + len(rims)), [one(2 * PS, PS)]
         )(counts, pos_z, pos_x, ext, probe, data, *tables)
 
-    grad, parts, rims = gradient(ext, probe)
+    grad, parts = gradient(ext, probe, [])
     ext, probe, info, info_all = call(
         exchange_kernel,
         [wide, square, small, small],
@@ -775,7 +777,7 @@
         ],
         1,
     )(grad, parts, packs, info, ext, goal, probe)
-    grad, parts, rims = gradient(ext, probe)
+    grad, parts, rims = gradient(ext, probe, [edge])
     every, phases = arr(ANG, ZS, TILES, WIDE), arr(ANG, TILES, 16, TW)
     psi_new, every, gathered, bases, cosines, sines = call(
         tail_kernel,

time: 73.3 us -> 73.4 us (level)
    pallas_call x2, Pallas kernels: 7.03 us -> 6.29 us  [gradient(): call(gradient_kernel, [wide, chunks] + rims, [SMEM] * 3 + [VMEM] * 7, [VM...]
where the time goes in v7:
time: 73.4 us; the launch traced here: 73.8 us
  Pallas kernels  71.7 us (98%)
  between operations  2.08 us (3%)
    pallas_call x1, Pallas kernels, shards(): call(exchange_kernel, [wide, square, small, small], [VMEM] * 7, [VMEM] *...  26.3 us
    pallas_call x1, Pallas kernels, shards(): call(tail_kernel, [edge, every, chunks, arr(ANG, 12, TILES, TW), phases,...  24.5 us
    pallas_call x1, Pallas kernels, shards(): call(image_kernel, [jax.ShapeDtypeStruct((2, ZS, YB, H), BF16), square, e...  9.16 us
    pallas_call x2, Pallas kernels, gradient(): call(gradient_kernel, [wide, chunks] + rims, [SMEM] * 3 + [VMEM] * 7, [VM...  6.29 us
    pallas_call x1, Pallas kernels, shards(): call(halo_kernel, outs, [SMEM] * 2 + [HBM] * 8, [VMEM] * len(outs), [one(...  5.42 us

profile of v7, /device:TPU:1, one launch (start us, length us, event | category | flops | bytes accessed | tf_op | source)
XLA Modules:
  0.0 73.8 jit_solution(1715432505387609110)
XLA Ops:
  0.6 0.0 copy-start.5
  0.6 0.0 copy-start.4
  2.0 5.4 %shard_map.175 = (f32[2,2,160,128]{3,2,1,0:T(8,128)S(1)}, f32[2,160,128]{2,1,0:T(8,128)S(1)}, f32[2,160,128]{2,1,0:T(8,128)S(1)}, f32[8,128]{1,0:T(8,128)S(1)}, ...) custom-call(s32[1,1]{1,0:T(1,128)S(6)} %copy.20.counts, ...), custom_call_target="tpu_custom_call" | custom-call | tf_op jit(solution)/shard_map/pallas_call | solution.py:750
  7.4 0.0 copy-done.5
  7.4 0.0 copy-done.4
  7.4 3.1 %shard_map.176 = (f32[2,2,160,128]{3,2,1,0:T(8,128)S(1)}, f32[8,32,128]{2,1,0:T(8,128)S(1)}) custom-call(s32[1,1]{1,0:T(1,128)S(6)} %copy.20.counts, s32[1,1,16]{2,1,0:T(1,128)S(1)} %copy-done.4, s32[1,1,16]{2,1,0:T(1,128)S(1)} %copy-done.5, f32[2,2,160,128]{3,2,1,0:T(8,128)S(1)} %get-tuple-element.31.ext.ext0, ...), custom_call_target="tpu_custom_call" | custom-call | tf_op jit(solution)/shard_map/pallas_call | solution.py:763
  10.5 0.0 copy-start.1
  10.5 0.0 copy-start.3
  10.5 26.3 %shard_map.177 = (f32[2,2,160,128]{3,2,1,0:T(8,128)S(1)}, f32[2,128,128]{2,1,0:T(8,128)S(1)}, f32[8,128]{1,0:T(8,128)S(1)}, f32[8,128]{1,0:T(8,128)S(1)}) custom-call(f32[2,2,160,128]{3,2,1,0:T(8,128)S(1)} %get-tuple-element.38.grad, f32[8,32,128]{2,1,0:T(8,128)S(1)} %get-tuple-element.39.parts, f32[2,160,128]{2,1,0:T(8,128)S(1)} %get-tuple-element.40.packs, ...), custom_call_target="tpu_custom_call" | custom-call | tf_op jit(solution)/shard_map/pallas_call | solution.py:768
  36.8 0.0 copy-start
  36.9 0.0 copy-start.2
  36.9 3.2 %shard_map.178 = (f32[2,2,160,128]{3,2,1,0:T(8,128)S(1)}, f32[8,32,128]{2,1,0:T(8,128)S(1)}, f32[2,160,128]{2,1,0:T(8,128)S(1)}) custom-call(s32[1,1]{1,0:T(1,128)S(6)} %copy.20.counts, s32[1,1,16]{2,1,0:T(1,128)S(1)} %copy-done.4, s32[1,1,16]{2,1,0:T(1,128)S(1)} %copy-done.5, f32[2,2,160,128]{3,2,1,0:T(8,128)S(1)} %get-tuple-element.43.ext, ...), custom_call_target="tpu_custom_call" | custom-call | tf_op jit(solution)/shard_map/pallas_call | solution.py:763
  40.1 0.0 copy-done.1
  40.1 0.0 copy-done.3
  40.1 24.5 %shard_map.179 = (f32[2,160,128]{2,1,0:T(8,128)S(1)}, f32[8,10,16,256]{3,2,1,0:T(8,128)S(1)}, f32[8,32,128]{2,1,0:T(8,128)S(1)}, f32[8,12,16,128]{3,2,1,0:T(8,12...) custom-call(f32[2,2,160,128]{3,2,1,0:T(8,128)S(1)} %get-tuple-element.43.ext, ...), custom_call_target="tpu_custom_call" | custom-call | tf_op jit(solution)/shard_map/pallas_call | solution.py:782
  64.6 0.0 copy-done
  64.6 0.0 copy-done.2
  64.6 9.2 %shard_map.180 = (bf16[2,10,32,2048]{3,2,1,0:T(8,128)(2,1)}, f32[2,128,128]{2,1,0:T(8,128)}, f32[2,160,128]{2,1,0:T(8,128)}) custom-call(f32[8,10,16,256]{3,2,1,0:T(8,128)S(1)} %get-tuple-element.49.rows, f32[8,12,16,128]{3,2,1,0:T(8,128)S(1)} %get-tuple-element.50.bases, f32[8,16,16,128]{3,2,1,0:T(8,128)S(1)} %get-tuple-element.51.cosines, ...), custom_call_target="tpu_custom_call" | custom-call | tf_op jit(solution)/shard_map/pallas_call | solution.py:798
Async XLA Ops:
  0.6 6.8 %copy-start.5 = (s32[1,1,16]{2,1,0:T(1,128)S(1)}, s32[1,1,16]{2,1,0:T(1,128)}, u32[]{:S(2)}) copy-start(s32[1,1,16]{2,1,0:T(1,128)} %pos_x.3) | copy-start | bytes 196
  0.6 6.8 %copy-start.4 = (s32[1,1,16]{2,1,0:T(1,128)S(1)}, s32[1,1,16]{2,1,0:T(1,128)}, u32[]{:S(2)}) copy-start(s32[1,1,16]{2,1,0:T(1,128)} %pos_z.3) | copy-start | bytes 196
  10.5 29.5 %copy-start.1 = (bf16[768,256]{1,0:T(8,128)(2,1)S(1)}, bf16[768,256]{1,0:T(8,128)(2,1)}, u32[]{:S(2)}) copy-start(bf16[768,256]{1,0:T(8,128)(2,1)} %constant.21.clone.right_f) | copy-start | bytes 1179652
  10.5 29.5 %copy-start.3 = (f32[2,16,128]{2,1,0:T(8,128)S(1)}, f32[2,16,128]{2,1,0:T(8,128)}, u32[]{:S(2)}) copy-start(f32[2,16,128]{2,1,0:T(8,128)} %constant.20.clone.turns) | copy-start | bytes 49156
  36.8 27.7 %copy-start = (bf16[768,256]{1,0:T(8,128)(2,1)S(1)}, bf16[768,256]{1,0:T(8,128)(2,1)}, u32[]{:S(2)}) copy-start(bf16[768,256]{1,0:T(8,128)(2,1)} %constant.23.clone.right_b) | copy-start | bytes 1179652
  36.9 27.7 %copy-start.2 = (f32[2,16,128]{2,1,0:T(8,128)S(1)}, f32[2,16,128]{2,1,0:T(8,128)}, u32[]{:S(2)}) copy-start(f32[2,16,128]{2,1,0:T(8,128)} %constant.22.clone.turns) | copy-start | bytes 49156

commit v8 on v7

--- a/solution.py
+++ b/solution.py
@@ -668,7 +668,7 @@
                 here = pl.ds(order * YB + 16 * group, 16)
                 value = (middle[here, pl.ds(0, TW)], middle[here, pl.ds(TW, TW)])
                 turn = (turns[0, pl.ds(order, 1), :], turns[1, pl.ds(order, 1), :])
-                items.append(times(value, turn))
+                items.append(times(value, turn) if order else value)
             for tile, item in enumerate(sixteen(items, 1)):
                 for part in range(2):
                     ready[slot, part, pl.ds(16 * group, 16), pl.ds(tile * TW, TW)] = item[part].astype(BF16)

time: 73.4 us -> 73.9 us (level)
  no operation moved by 1% of the time
where the time goes in v8:
time: 73.9 us; the launch traced here: 74 us
  Pallas kernels  71.9 us (97%)
  between operations  2.08 us (3%)
    pallas_call x1, Pallas kernels, shards(): call(exchange_kernel, [wide, square, small, small], [VMEM] * 7, [VMEM] *...  26.3 us
    pallas_call x1, Pallas kernels, shards(): call(tail_kernel, [edge, every, chunks, arr(ANG, 12, TILES, TW), phases,...  24.8 us
    pallas_call x1, Pallas kernels, shards(): call(image_kernel, [jax.ShapeDtypeStruct((2, ZS, YB, H), BF16), square, e...  9.17 us
    pallas_call x2, Pallas kernels, gradient(): call(gradient_kernel, [wide, chunks] + rims, [SMEM] * 3 + [VMEM] * 7, [VM...  6.24 us
    pallas_call x1, Pallas kernels, shards(): call(halo_kernel, outs, [SMEM] * 2 + [HBM] * 8, [VMEM] * len(outs), [one(...  5.42 us

profile of v8, /device:TPU:1, one launch (start us, length us, event | category | flops | bytes accessed | tf_op | source)
XLA Modules:
  0.0 74.0 jit_solution(13994799054302167981)
XLA Ops:
  0.6 0.0 copy-start.5
  0.6 0.0 copy-start.4
  2.0 5.4 %shard_map.175 = (f32[2,2,160,128]{3,2,1,0:T(8,128)S(1)}, f32[2,160,128]{2,1,0:T(8,128)S(1)}, f32[2,160,128]{2,1,0:T(8,128)S(1)}, f32[8,128]{1,0:T(8,128)S(1)}, ...) custom-call(s32[1,1]{1,0:T(1,128)S(6)} %copy.20.counts, ...), custom_call_target="tpu_custom_call" | custom-call | tf_op jit(solution)/shard_map/pallas_call | solution.py:750
  7.4 0.0 copy-done.5
  7.4 0.0 copy-done.4
  7.4 3.1 %shard_map.176 = (f32[2,2,160,128]{3,2,1,0:T(8,128)S(1)}, f32[8,32,128]{2,1,0:T(8,128)S(1)}) custom-call(s32[1,1]{1,0:T(1,128)S(6)} %copy.20.counts, s32[1,1,16]{2,1,0:T(1,128)S(1)} %copy-done.4, s32[1,1,16]{2,1,0:T(1,128)S(1)} %copy-done.5, f32[2,2,160,128]{3,2,1,0:T(8,128)S(1)} %get-tuple-element.31.ext.ext0, ...), custom_call_target="tpu_custom_call" | custom-call | tf_op jit(solution)/shard_map/pallas_call | solution.py:763
  10.5 0.0 copy-start.1
  10.5 0.0 copy-start.3
  10.5 26.3 %shard_map.177 = (f32[2,2,160,128]{3,2,1,0:T(8,128)S(1)}, f32[2,128,128]{2,1,0:T(8,128)S(1)}, f32[8,128]{1,0:T(8,128)S(1)}, f32[8,128]{1,0:T(8,128)S(1)}) custom-call(f32[2,2,160,128]{3,2,1,0:T(8,128)S(1)} %get-tuple-element.38.grad, f32[8,32,128]{2,1,0:T(8,128)S(1)} %get-tuple-element.39.parts, f32[2,160,128]{2,1,0:T(8,128)S(1)} %get-tuple-element.40.packs, ...), custom_call_target="tpu_custom_call" | custom-call | tf_op jit(solution)/shard_map/pallas_call | solution.py:768
  36.8 0.0 copy-start
  36.8 0.0 copy-start.2
  36.8 3.2 %shard_map.178 = (f32[2,2,160,128]{3,2,1,0:T(8,128)S(1)}, f32[8,32,128]{2,1,0:T(8,128)S(1)}, f32[2,160,128]{2,1,0:T(8,128)S(1)}) custom-call(s32[1,1]{1,0:T(1,128)S(6)} %copy.20.counts, s32[1,1,16]{2,1,0:T(1,128)S(1)} %copy-done.4, s32[1,1,16]{2,1,0:T(1,128)S(1)} %copy-done.5, f32[2,2,160,128]{3,2,1,0:T(8,128)S(1)} %get-tuple-element.43.ext, ...), custom_call_target="tpu_custom_call" | custom-call | tf_op jit(solution)/shard_map/pallas_call | solution.py:763
  40.0 0.0 copy-done.1
  40.0 0.0 copy-done.3
  40.0 24.8 %shard_map.179 = (f32[2,160,128]{2,1,0:T(8,128)S(1)}, f32[8,10,16,256]{3,2,1,0:T(8,128)S(1)}, f32[8,32,128]{2,1,0:T(8,128)S(1)}, f32[8,12,16,128]{3,2,1,0:T(8,12...) custom-call(f32[2,2,160,128]{3,2,1,0:T(8,128)S(1)} %get-tuple-element.43.ext, ...), custom_call_target="tpu_custom_call" | custom-call | tf_op jit(solution)/shard_map/pallas_call | solution.py:782
  64.8 0.0 copy-done
  64.8 0.0 copy-done.2
  64.8 9.2 %shard_map.180 = (bf16[2,10,32,2048]{3,2,1,0:T(8,128)(2,1)}, f32[2,128,128]{2,1,0:T(8,128)}, f32[2,160,128]{2,1,0:T(8,128)}) custom-call(f32[8,10,16,256]{3,2,1,0:T(8,128)S(1)} %get-tuple-element.49.rows, f32[8,12,16,128]{3,2,1,0:T(8,128)S(1)} %get-tuple-element.50.bases, f32[8,16,16,128]{3,2,1,0:T(8,128)S(1)} %get-tuple-element.51.cosines, ...), custom_call_target="tpu_custom_call" | custom-call | tf_op jit(solution)/shard_map/pallas_call | solution.py:798
Async XLA Ops:
  0.6 6.8 %copy-start.5 = (s32[1,1,16]{2,1,0:T(1,128)S(1)}, s32[1,1,16]{2,1,0:T(1,128)}, u32[]{:S(2)}) copy-start(s32[1,1,16]{2,1,0:T(1,128)} %pos_x.3) | copy-start | bytes 196
  0.6 6.8 %copy-start.4 = (s32[1,1,16]{2,1,0:T(1,128)S(1)}, s32[1,1,16]{2,1,0:T(1,128)}, u32[]{:S(2)}) copy-start(s32[1,1,16]{2,1,0:T(1,128)} %pos_z.3) | copy-start | bytes 196
  10.5 29.5 %copy-start.1 = (bf16[768,256]{1,0:T(8,128)(2,1)S(1)}, bf16[768,256]{1,0:T(8,128)(2,1)}, u32[]{:S(2)}) copy-start(bf16[768,256]{1,0:T(8,128)(2,1)} %constant.21.clone.right_f) | copy-start | bytes 1179652
  10.5 29.5 %copy-start.3 = (f32[2,16,128]{2,1,0:T(8,128)S(1)}, f32[2,16,128]{2,1,0:T(8,128)}, u32[]{:S(2)}) copy-start(f32[2,16,128]{2,1,0:T(8,128)} %constant.20.clone.turns) | copy-start | bytes 49156
  36.8 28.0 %copy-start = (bf16[768,256]{1,0:T(8,128)(2,1)S(1)}, bf16[768,256]{1,0:T(8,128)(2,1)}, u32[]{:S(2)}) copy-start(bf16[768,256]{1,0:T(8,128)(2,1)} %constant.23.clone.right_b) | copy-start | bytes 1179652
  36.8 28.0 %copy-start.2 = (f32[2,16,128]{2,1,0:T(8,128)S(1)}, f32[2,16,128]{2,1,0:T(8,128)}, u32[]{:S(2)}) copy-start(f32[2,16,128]{2,1,0:T(8,128)} %constant.22.clone.turns) | copy-start | bytes 49156
